TPU v7x, 128 devices: a whole 4x4x4 slice. The times are simulated.
128 devices in a mesh: section: 8 (over x_lo, z), fsdp: 16 (over y, x_hi, core).
Axes of the slice: x: 4 (x_hi: 2, x_lo: 2; x = x_hi * 2 + x_lo), y: 4, z: 4, core: 2. Of those that a mesh axis runs over, the one named last changes fastest.
Arguments:
- feats: bfloat16 [4, 16, 256, 1536], P(None, 'fsdp'), may hold values from -6 to 6
- w_in: bfloat16 [2, 8, 1536, 3072], P(None, 'section', 'fsdp'), may hold values from -0.15625 to 0.15625
- dw_kernel: bfloat16 [2, 8, 31, 1536], P(None, 'section', None, 'fsdp'), may hold values from -1 to 1
- mask_embed: bfloat16 [1536], replicated, may hold values from -6 to 6
- w_ctx: bfloat16 [1536, 768], replicated, may hold values from -0.15625 to 0.15625
- w_tgt: bfloat16 [1536, 768], replicated, may hold values from -0.15625 to 0.15625
- mask_starts: int32 [4, 16, 12], P(None, 'fsdp'), may hold values from 0 to 246
- distractors: int32 [4, 16, 256, 100], P(None, 'fsdp', 'section'), may hold values from 0 to 255
Outputs:
- frame_loss: float32 [4, 16, 256], P(None, 'fsdp', 'section')
All inputs are finite; a program needn't handle non-finite values.
Results may differ from a plain program's by a relative error of at most 0.0054.
Values may be sent and summed in bfloat16 or wider, within the bound.
A program may use at most 128 MiB of HBM per device.

v0:
```python
import jax
import jax.numpy as jnp
from jax import lax
from jax.sharding import PartitionSpec as P

MASK_LEN = 10


def passed_along(block, axis, distance):
    devices = range(lax.axis_size(axis))
    route = [((i - distance) % len(devices), i) for i in devices]
    return lax.ppermute(block, axis, route)


def spread_2(value, axis, source):
    kept = jnp.where(lax.axis_index(axis) == source, value, 0).astype(value.dtype)
    return lax.psum(kept, axis)


def conv_module(frames_in, weight, kernel):
    width = frames_in.shape[1]
    frames = frames_in.shape[0]
    values = frames_in.astype(jnp.float32)
    center = jnp.mean(values, axis=1, keepdims=True)
    spread = jnp.mean((values - center) ** 2, axis=1, keepdims=True)
    normed = ((values - center) * lax.rsqrt(spread + 1e-05)).astype(jnp.bfloat16)
    proj = jnp.dot(normed, weight, preferred_element_type=jnp.float32)
    glu = (proj[:, :width] * jax.nn.sigmoid(proj[:, width:])).astype(jnp.bfloat16)
    taps = kernel.shape[0]
    half = taps // 2
    padded = jnp.pad(glu, ((half, half), (0, 0)))
    mixed = jnp.zeros(values.shape, jnp.float32)
    for tap in range(taps):
        mixed = mixed + padded[tap : tap + frames, :].astype(jnp.float32) * kernel[tap].astype(
            jnp.float32
        )
    return (values + jax.nn.silu(mixed)).astype(jnp.bfloat16)


def unit_rows(values):
    return (values * lax.rsqrt(jnp.sum(values * values, axis=-1, keepdims=True) + 1e-06)).astype(
        jnp.bfloat16
    )


def score_rows(ctx_rows, tgt, rows, picks):
    spots = jnp.arange(tgt.shape[1], dtype=jnp.int32)

    def one_batch(items):
        ctx_one, tgt_one, pick_one = items
        sims = jnp.dot(ctx_one, tgt_one.T, preferred_element_type=jnp.float32)
        positive = jnp.sum(jnp.where(spots[None, :] == rows[:, None], sims, 0.0), axis=1) * 10.0
        negative = (
            jnp.sum(jnp.where(pick_one[..., None] == spots, sims[:, None, :], 0.0), axis=2) * 10.0
        )
        total = jnp.exp(positive) + jnp.sum(jnp.exp(negative), axis=1)
        return jnp.log(total) - positive

    return lax.map(one_batch, (ctx_rows, tgt, picks))


def on_device(feats, w_in, dw_kernel, mask_embed, w_ctx, w_tgt, mask_starts, distractors):
    sections = lax.axis_size("section")
    section = lax.axis_index("section")
    micro = feats.shape[0]
    frames = feats.shape[2]
    repeats = w_in.shape[0]
    feats_local = feats[:, 0]
    spots = jnp.arange(frames, dtype=jnp.int32)
    starts = mask_starts[:, 0][:, :, None]
    covered = jnp.any(
        (spots[None, None, :] >= starts) & (spots[None, None, :] < starts + MASK_LEN), axis=1
    )
    masked_in = jnp.where(covered[:, :, None], mask_embed[None, None, :], feats_local)
    weight_rows = w_in[:, 0]
    kernel_cols = dw_kernel[:, 0]
    total_steps = repeats * sections + micro - 1

    def advance(step, state, finished, full_w, full_k):
        offset = step - section
        cycle = jnp.maximum(offset, 0)
        slot = cycle % sections
        turn = cycle // sections
        valid = (offset >= 0) & (slot < micro) & (turn < repeats)
        slot_idx = jnp.minimum(slot, micro - 1)
        turn_idx = jnp.minimum(turn, full_w.shape[0] - 1)
        fresh = lax.dynamic_index_in_dim(masked_in, slot_idx, 0, keepdims=False)
        incoming = jnp.where((section == 0) & (turn == 0), fresh, state)
        result = lax.cond(
            valid,
            lambda: conv_module(
                incoming,
                lax.dynamic_index_in_dim(full_w, turn_idx, 0, keepdims=False),
                lax.dynamic_index_in_dim(full_k, turn_idx, 0, keepdims=False),
            ),
            lambda: incoming,
        )
        write = valid & (section == sections - 1) & (turn == repeats - 1)
        updated = lax.dynamic_update_index_in_dim(finished, result, slot_idx, 0)
        finished = jnp.where(write, updated, finished)
        return (result, finished)

    carry = (
        jnp.zeros((frames, feats.shape[3]), jnp.bfloat16),
        jnp.zeros((micro, frames, feats.shape[3]), jnp.bfloat16),
    )
    full_w, full_k = (
        lax.all_gather(weight_rows, "fsdp", axis=1, tiled=True),
        lax.all_gather(kernel_cols, "fsdp", axis=2, tiled=True),
    )

    def loop_step(step, pair):
        result, finished = advance(step, pair[0], pair[1], full_w, full_k)
        moved = passed_along(result, "section", 1)
        return (moved, finished)

    carry = lax.fori_loop(0, total_steps - 1, loop_step, carry)
    unused, finished = advance(total_steps - 1, carry[0], carry[1], full_w, full_k)
    share = frames // sections
    rows = section * share + jnp.arange(share, dtype=jnp.int32)
    tgt = unit_rows(
        jnp.einsum("mjd,de->mje", feats_local, w_tgt, preferred_element_type=jnp.float32)
    )
    picks = distractors[:, 0]
    whole = spread_2(finished, "section", sections - 1)
    encoded = lax.dynamic_slice_in_dim(whole, section * share, share, 1)
    ctx = unit_rows(jnp.einsum("mfd,de->mfe", encoded, w_ctx, preferred_element_type=jnp.float32))
    frame_loss = score_rows(ctx, tgt, rows, picks)
    return frame_loss[:, None, :]


def solution(mesh):
    placed = (
        P(None, "fsdp", None, None),
        P(None, "section", "fsdp", None),
        P(None, "section", None, "fsdp"),
        P(),
        P(),
        P(),
        P(None, "fsdp", None),
        P(None, "fsdp", "section", None),
    )
    return jax.shard_map(
        on_device, mesh=mesh, in_specs=placed, out_specs=P(None, "fsdp", "section"), check_vma=False
    )
```

profile of v0, /device:TPU:1, one launch (start us, length us, event | category | flops | bytes accessed | tf_op | source)
XLA Modules:
  0.0 1097.6 jit_solution(15545361774053649678)
XLA Ops:
  9.7 32.6 %all-gather.1 = bf16[2,1,31,1536]{2,0,1,3:T(2,128)(2,1)S(1)} all-gather(bf16[2,1,31,96]{2,0,1,3:T(2,128)(2,1)S(1)} %copy.30), channel_id=3, replica_groups=mesh['section'=8,'fsdp'=16] {'fsdp'}, dimensions={3}, use_global_device_ids=true | all-gather | bytes 202368 | tf_op jit(solution)/shard_map/all_gather | solution.py:109
  46.9 88.1 %all-gather.4.cloned.1.call-done = bf16[2,1,1536,3072]{3,2,0,1:T(8,128)(2,1)} async-done(((bf16[2,1,96,3072]{3,2,0,1:T(8,128)(2,1)}), bf16[2,1,1536,3072]{3,2,0,1:T(8,128)(2,1)}) %all-gather.4.cloned.1.call-update) | async-done | bytes 18874384 | tf_op jit(solution)/shard_map/all_gather | solution.py:108
  137.9 815.1 %while.29 = (s32[]{:T(128)}, bf16[256,1536]{1,0:T(8,128)(2,1)}, bf16[4,256,1536]{2,1,0:T(8,128)(2,1)}, s32[]{:T(128)}, pred[]{:T(512)}, /*index=5*/bf16[4,256,15...) while((s32[]{:T(128)}, bf16[256,1536]{1,0:T(8,128)(2,1)}, ...), condition=%wide.region_6.7_spmd, body=%wide.region_1.6_spmd.sunk | while | flops 2461580032 | bytes 29584392 | solution.py:117
  139.2 29.7 %conditional.4 = (bf16[256,1536]{1,0:T(8,128)(2,1)S(1)}) conditional(s32[]{:T(128)} %convert_element_type.1272, bf16[256,1536]{1,0:T(8,128)(2,1)S(1)} %bitcast_select_fusion.5, (bf16[256,1536]{1,0:T(8,128)(2,1)S(1)}, s32[]{:T(128)}, bf16[2,1536,3072]{2,1,0:T(8,128)(2,1)}, bf16[2,31,1536]{2,1,0:T(8,128)(2,1)S(1)}) %tuple.165), branch_computations={%region_2.2_spmd, %region_3.5_spmd} | conditional | flops 2460793600 | bytes 21719586 | solution.py:89
  147.0 21.9 %fusion.19 = bf16[256,1536]{1,0:T(8,128)(2,1)S(1)} fusion(bf16[256,1536]{1,0:T(8,128)(2,1)S(1)} %get-tuple-element.263, bf16[256,1536]{1,0:T(8,128)(2,1)} %fusion.24, f32[1536]{0:T(1024)S(1)} %get-tuple-element.400, f32[1536]{0:T(1024)S(1)} %get-tuple-element.371, f32[1536]{0:T(1024)S(1)} %get-tuple-element.372, f32[1536]{0:T(1024)S(1)} %get-tuple-element.373, ...), kind=kLoop, calls=%fused_computation.29 | loop fusion | flops 38928384 | bytes 2549760 | tf_op jit(solution)/shard_map/while/body/eval_jaxpr/cond/branch_1_fun/convert_element_type | solution.py:37
  171.2 18.9 %collective-permute-done = bf16[256,1536]{1,0:T(8,128)(2,1)} collective-permute-done((bf16[256,1536]{1,0:T(8,128)(2,1)S(1)}, bf16[256,1536]{1,0:T(8,128)(2,1)}, u32[]{:S(2)}, u32[]{:S(2)}) %collective-permute-start) | collective-permute-done | bytes 786464 | tf_op jit(solution)/shard_map/while/body/eval_jaxpr/ppermute | solution.py:12
  191.3 29.7 %conditional.4 = (bf16[256,1536]{1,0:T(8,128)(2,1)S(1)}) conditional(s32[]{:T(128)} %convert_element_type.1272, bf16[256,1536]{1,0:T(8,128)(2,1)S(1)} %bitcast_select_fusion.5, (bf16[256,1536]{1,0:T(8,128)(2,1)S(1)}, s32[]{:T(128)}, bf16[2,1536,3072]{2,1,0:T(8,128)(2,1)}, bf16[2,31,1536]{2,1,0:T(8,128)(2,1)S(1)}) %tuple.165), branch_computations={%region_2.2_spmd, %region_3.5_spmd} | conditional | flops 2460793600 | bytes 21719586 | solution.py:89
  199.0 21.9 %fusion.19 = bf16[256,1536]{1,0:T(8,128)(2,1)S(1)} fusion(bf16[256,1536]{1,0:T(8,128)(2,1)S(1)} %get-tuple-element.263, bf16[256,1536]{1,0:T(8,128)(2,1)} %fusion.24, f32[1536]{0:T(1024)S(1)} %get-tuple-element.400, f32[1536]{0:T(1024)S(1)} %get-tuple-element.371, f32[1536]{0:T(1024)S(1)} %get-tuple-element.372, f32[1536]{0:T(1024)S(1)} %get-tuple-element.373, ...), kind=kLoop, calls=%fused_computation.29 | loop fusion | flops 38928384 | bytes 2549760 | tf_op jit(solution)/shard_map/while/body/eval_jaxpr/cond/branch_1_fun/convert_element_type | solution.py:37
  223.3 17.9 %collective-permute-done = bf16[256,1536]{1,0:T(8,128)(2,1)} collective-permute-done((bf16[256,1536]{1,0:T(8,128)(2,1)S(1)}, bf16[256,1536]{1,0:T(8,128)(2,1)}, u32[]{:S(2)}, u32[]{:S(2)}) %collective-permute-start) | collective-permute-done | bytes 786464 | tf_op jit(solution)/shard_map/while/body/eval_jaxpr/ppermute | solution.py:12
  242.4 29.7 %conditional.4 = (bf16[256,1536]{1,0:T(8,128)(2,1)S(1)}) conditional(s32[]{:T(128)} %convert_element_type.1272, bf16[256,1536]{1,0:T(8,128)(2,1)S(1)} %bitcast_select_fusion.5, (bf16[256,1536]{1,0:T(8,128)(2,1)S(1)}, s32[]{:T(128)}, bf16[2,1536,3072]{2,1,0:T(8,128)(2,1)}, bf16[2,31,1536]{2,1,0:T(8,128)(2,1)S(1)}) %tuple.165), branch_computations={%region_2.2_spmd, %region_3.5_spmd} | conditional | flops 2460793600 | bytes 21719586 | solution.py:89
  250.2 21.9 %fusion.19 = bf16[256,1536]{1,0:T(8,128)(2,1)S(1)} fusion(bf16[256,1536]{1,0:T(8,128)(2,1)S(1)} %get-tuple-element.263, bf16[256,1536]{1,0:T(8,128)(2,1)} %fusion.24, f32[1536]{0:T(1024)S(1)} %get-tuple-element.400, f32[1536]{0:T(1024)S(1)} %get-tuple-element.371, f32[1536]{0:T(1024)S(1)} %get-tuple-element.372, f32[1536]{0:T(1024)S(1)} %get-tuple-element.373, ...), kind=kLoop, calls=%fused_computation.29 | loop fusion | flops 38928384 | bytes 2549760 | tf_op jit(solution)/shard_map/while/body/eval_jaxpr/cond/branch_1_fun/convert_element_type | solution.py:37
  274.4 17.0 %collective-permute-done = bf16[256,1536]{1,0:T(8,128)(2,1)} collective-permute-done((bf16[256,1536]{1,0:T(8,128)(2,1)S(1)}, bf16[256,1536]{1,0:T(8,128)(2,1)}, u32[]{:S(2)}, u32[]{:S(2)}) %collective-permute-start) | collective-permute-done | bytes 786464 | tf_op jit(solution)/shard_map/while/body/eval_jaxpr/ppermute | solution.py:12
  292.7 29.7 %conditional.4 = (bf16[256,1536]{1,0:T(8,128)(2,1)S(1)}) conditional(s32[]{:T(128)} %convert_element_type.1272, bf16[256,1536]{1,0:T(8,128)(2,1)S(1)} %bitcast_select_fusion.5, (bf16[256,1536]{1,0:T(8,128)(2,1)S(1)}, s32[]{:T(128)}, bf16[2,1536,3072]{2,1,0:T(8,128)(2,1)}, bf16[2,31,1536]{2,1,0:T(8,128)(2,1)S(1)}) %tuple.165), branch_computations={%region_2.2_spmd, %region_3.5_spmd} | conditional | flops 2460793600 | bytes 21719586 | solution.py:89
  300.5 21.9 %fusion.19 = bf16[256,1536]{1,0:T(8,128)(2,1)S(1)} fusion(bf16[256,1536]{1,0:T(8,128)(2,1)S(1)} %get-tuple-element.263, bf16[256,1536]{1,0:T(8,128)(2,1)} %fusion.24, f32[1536]{0:T(1024)S(1)} %get-tuple-element.400, f32[1536]{0:T(1024)S(1)} %get-tuple-element.371, f32[1536]{0:T(1024)S(1)} %get-tuple-element.372, f32[1536]{0:T(1024)S(1)} %get-tuple-element.373, ...), kind=kLoop, calls=%fused_computation.29 | loop fusion | flops 38928384 | bytes 2549760 | tf_op jit(solution)/shard_map/while/body/eval_jaxpr/cond/branch_1_fun/convert_element_type | solution.py:37
  324.7 16.1 %collective-permute-done = bf16[256,1536]{1,0:T(8,128)(2,1)} collective-permute-done((bf16[256,1536]{1,0:T(8,128)(2,1)S(1)}, bf16[256,1536]{1,0:T(8,128)(2,1)}, u32[]{:S(2)}, u32[]{:S(2)}) %collective-permute-start) | collective-permute-done | bytes 786464 | tf_op jit(solution)/shard_map/while/body/eval_jaxpr/ppermute | solution.py:12
  342.0 28.2 %collective-permute-start = (bf16[256,1536]{1,0:T(8,128)(2,1)S(1)}, bf16[256,1536]{1,0:T(8,128)(2,1)}, u32[]{:S(2)}, u32[]{:S(2)}) collective-permute-start(bf16[256,1536]{1,0:T(8,128)(2,1)S(1)} %get-tuple-element.645), channel_id=1, source_target_pairs={{112,0},{0,16},{16,32},{32,48},{48,64},{64,80},{80,96},{96,112},{1... | collective-permute-start | bytes 2359304 | tf_op jit(solution)/shard_map/while/body/eval_jaxpr/ppermute | solution.py:12
  372.4 11.1 %collective-permute-done = bf16[256,1536]{1,0:T(8,128)(2,1)} collective-permute-done((bf16[256,1536]{1,0:T(8,128)(2,1)S(1)}, bf16[256,1536]{1,0:T(8,128)(2,1)}, u32[]{:S(2)}, u32[]{:S(2)}) %collective-permute-start) | collective-permute-done | bytes 786464 | tf_op jit(solution)/shard_map/while/body/eval_jaxpr/ppermute | solution.py:12
  389.5 12.0 %collective-permute-done = bf16[256,1536]{1,0:T(8,128)(2,1)} collective-permute-done((bf16[256,1536]{1,0:T(8,128)(2,1)S(1)}, bf16[256,1536]{1,0:T(8,128)(2,1)}, u32[]{:S(2)}, u32[]{:S(2)}) %collective-permute-start) | collective-permute-done | bytes 786464 | tf_op jit(solution)/shard_map/while/body/eval_jaxpr/ppermute | solution.py:12
  402.8 28.7 %collective-permute-start = (bf16[256,1536]{1,0:T(8,128)(2,1)S(1)}, bf16[256,1536]{1,0:T(8,128)(2,1)}, u32[]{:S(2)}, u32[]{:S(2)}) collective-permute-start(bf16[256,1536]{1,0:T(8,128)(2,1)S(1)} %get-tuple-element.645), channel_id=1, source_target_pairs={{112,0},{0,16},{16,32},{32,48},{48,64},{64,80},{80,96},{96,112},{1... | collective-permute-start | bytes 2359304 | tf_op jit(solution)/shard_map/while/body/eval_jaxpr/ppermute | solution.py:12
  433.7 9.2 collective-permute-done
  449.7 71.2 %collective-permute-done = bf16[256,1536]{1,0:T(8,128)(2,1)} collective-permute-done((bf16[256,1536]{1,0:T(8,128)(2,1)S(1)}, bf16[256,1536]{1,0:T(8,128)(2,1)}, u32[]{:S(2)}, u32[]{:S(2)}) %collective-permute-start) | collective-permute-done | bytes 786464 | tf_op jit(solution)/shard_map/while/body/eval_jaxpr/ppermute | solution.py:12
  522.3 29.7 %conditional.4 = (bf16[256,1536]{1,0:T(8,128)(2,1)S(1)}) conditional(s32[]{:T(128)} %convert_element_type.1272, bf16[256,1536]{1,0:T(8,128)(2,1)S(1)} %bitcast_select_fusion.5, (bf16[256,1536]{1,0:T(8,128)(2,1)S(1)}, s32[]{:T(128)}, bf16[2,1536,3072]{2,1,0:T(8,128)(2,1)}, bf16[2,31,1536]{2,1,0:T(8,128)(2,1)S(1)}) %tuple.165), branch_computations={%region_2.2_spmd, %region_3.5_spmd} | conditional | flops 2460793600 | bytes 21719586 | solution.py:89
  522.9 5.3 fusion.12
  530.1 21.9 %fusion.19 = bf16[256,1536]{1,0:T(8,128)(2,1)S(1)} fusion(bf16[256,1536]{1,0:T(8,128)(2,1)S(1)} %get-tuple-element.263, bf16[256,1536]{1,0:T(8,128)(2,1)} %fusion.24, f32[1536]{0:T(1024)S(1)} %get-tuple-element.400, f32[1536]{0:T(1024)S(1)} %get-tuple-element.371, f32[1536]{0:T(1024)S(1)} %get-tuple-element.372, f32[1536]{0:T(1024)S(1)} %get-tuple-element.373, ...), kind=kLoop, calls=%fused_computation.29 | loop fusion | flops 38928384 | bytes 2549760 | tf_op jit(solution)/shard_map/while/body/eval_jaxpr/cond/branch_1_fun/convert_element_type | solution.py:37
  554.3 13.8 %collective-permute-done = bf16[256,1536]{1,0:T(8,128)(2,1)} collective-permute-done((bf16[256,1536]{1,0:T(8,128)(2,1)S(1)}, bf16[256,1536]{1,0:T(8,128)(2,1)}, u32[]{:S(2)}, u32[]{:S(2)}) %collective-permute-start) | collective-permute-done | bytes 786464 | tf_op jit(solution)/shard_map/while/body/eval_jaxpr/ppermute | solution.py:12
  569.6 29.7 %conditional.4 = (bf16[256,1536]{1,0:T(8,128)(2,1)S(1)}) conditional(s32[]{:T(128)} %convert_element_type.1272, bf16[256,1536]{1,0:T(8,128)(2,1)S(1)} %bitcast_select_fusion.5, (bf16[256,1536]{1,0:T(8,128)(2,1)S(1)}, s32[]{:T(128)}, bf16[2,1536,3072]{2,1,0:T(8,128)(2,1)}, bf16[2,31,1536]{2,1,0:T(8,128)(2,1)S(1)}) %tuple.165), branch_computations={%region_2.2_spmd, %region_3.5_spmd} | conditional | flops 2460793600 | bytes 21719586 | solution.py:89
  570.2 5.3 fusion.12
  577.5 21.9 %fusion.19 = bf16[256,1536]{1,0:T(8,128)(2,1)S(1)} fusion(bf16[256,1536]{1,0:T(8,128)(2,1)S(1)} %get-tuple-element.263, bf16[256,1536]{1,0:T(8,128)(2,1)} %fusion.24, f32[1536]{0:T(1024)S(1)} %get-tuple-element.400, f32[1536]{0:T(1024)S(1)} %get-tuple-element.371, f32[1536]{0:T(1024)S(1)} %get-tuple-element.372, f32[1536]{0:T(1024)S(1)} %get-tuple-element.373, ...), kind=kLoop, calls=%fused_computation.29 | loop fusion | flops 38928384 | bytes 2549760 | tf_op jit(solution)/shard_map/while/body/eval_jaxpr/cond/branch_1_fun/convert_element_type | solution.py:37
  601.7 12.9 %collective-permute-done = bf16[256,1536]{1,0:T(8,128)(2,1)} collective-permute-done((bf16[256,1536]{1,0:T(8,128)(2,1)S(1)}, bf16[256,1536]{1,0:T(8,128)(2,1)}, u32[]{:S(2)}, u32[]{:S(2)}) %collective-permute-start) | collective-permute-done | bytes 786464 | tf_op jit(solution)/shard_map/while/body/eval_jaxpr/ppermute | solution.py:12
  616.0 29.7 %conditional.4 = (bf16[256,1536]{1,0:T(8,128)(2,1)S(1)}) conditional(s32[]{:T(128)} %convert_element_type.1272, bf16[256,1536]{1,0:T(8,128)(2,1)S(1)} %bitcast_select_fusion.5, (bf16[256,1536]{1,0:T(8,128)(2,1)S(1)}, s32[]{:T(128)}, bf16[2,1536,3072]{2,1,0:T(8,128)(2,1)}, bf16[2,31,1536]{2,1,0:T(8,128)(2,1)S(1)}) %tuple.165), branch_computations={%region_2.2_spmd, %region_3.5_spmd} | conditional | flops 2460793600 | bytes 21719586 | solution.py:89
  616.6 5.3 fusion.12
  623.9 21.9 %fusion.19 = bf16[256,1536]{1,0:T(8,128)(2,1)S(1)} fusion(bf16[256,1536]{1,0:T(8,128)(2,1)S(1)} %get-tuple-element.263, bf16[256,1536]{1,0:T(8,128)(2,1)} %fusion.24, f32[1536]{0:T(1024)S(1)} %get-tuple-element.400, f32[1536]{0:T(1024)S(1)} %get-tuple-element.371, f32[1536]{0:T(1024)S(1)} %get-tuple-element.372, f32[1536]{0:T(1024)S(1)} %get-tuple-element.373, ...), kind=kLoop, calls=%fused_computation.29 | loop fusion | flops 38928384 | bytes 2549760 | tf_op jit(solution)/shard_map/while/body/eval_jaxpr/cond/branch_1_fun/convert_element_type | solution.py:37
  648.1 12.0 %collective-permute-done = bf16[256,1536]{1,0:T(8,128)(2,1)} collective-permute-done((bf16[256,1536]{1,0:T(8,128)(2,1)S(1)}, bf16[256,1536]{1,0:T(8,128)(2,1)}, u32[]{:S(2)}, u32[]{:S(2)}) %collective-permute-start) | collective-permute-done | bytes 786464 | tf_op jit(solution)/shard_map/while/body/eval_jaxpr/ppermute | solution.py:12
  661.5 29.7 %conditional.4 = (bf16[256,1536]{1,0:T(8,128)(2,1)S(1)}) conditional(s32[]{:T(128)} %convert_element_type.1272, bf16[256,1536]{1,0:T(8,128)(2,1)S(1)} %bitcast_select_fusion.5, (bf16[256,1536]{1,0:T(8,128)(2,1)S(1)}, s32[]{:T(128)}, bf16[2,1536,3072]{2,1,0:T(8,128)(2,1)}, bf16[2,31,1536]{2,1,0:T(8,128)(2,1)S(1)}) %tuple.165), branch_computations={%region_2.2_spmd, %region_3.5_spmd} | conditional | flops 2460793600 | bytes 21719586 | solution.py:89
  662.1 5.3 fusion.12
  669.3 21.9 %fusion.19 = bf16[256,1536]{1,0:T(8,128)(2,1)S(1)} fusion(bf16[256,1536]{1,0:T(8,128)(2,1)S(1)} %get-tuple-element.263, bf16[256,1536]{1,0:T(8,128)(2,1)} %fusion.24, f32[1536]{0:T(1024)S(1)} %get-tuple-element.400, f32[1536]{0:T(1024)S(1)} %get-tuple-element.371, f32[1536]{0:T(1024)S(1)} %get-tuple-element.372, f32[1536]{0:T(1024)S(1)} %get-tuple-element.373, ...), kind=kLoop, calls=%fused_computation.29 | loop fusion | flops 38928384 | bytes 2549760 | tf_op jit(solution)/shard_map/while/body/eval_jaxpr/cond/branch_1_fun/convert_element_type | solution.py:37
  693.5 10.8 collective-permute-done
  705.8 28.2 %collective-permute-start = (bf16[256,1536]{1,0:T(8,128)(2,1)S(1)}, bf16[256,1536]{1,0:T(8,128)(2,1)}, u32[]{:S(2)}, u32[]{:S(2)}) collective-permute-start(bf16[256,1536]{1,0:T(8,128)(2,1)S(1)} %get-tuple-element.645), channel_id=1, source_target_pairs={{112,0},{0,16},{16,32},{32,48},{48,64},{64,80},{80,96},{96,112},{1... | collective-permute-start | bytes 2359304 | tf_op jit(solution)/shard_map/while/body/eval_jaxpr/ppermute | solution.py:12
  736.2 6.7 collective-permute-done
  748.7 11.7 %collective-permute-done = bf16[256,1536]{1,0:T(8,128)(2,1)} collective-permute-done((bf16[256,1536]{1,0:T(8,128)(2,1)S(1)}, bf16[256,1536]{1,0:T(8,128)(2,1)}, u32[]{:S(2)}, u32[]{:S(2)}) %collective-permute-start) | collective-permute-done | bytes 786464 | tf_op jit(solution)/shard_map/while/body/eval_jaxpr/ppermute | solution.py:12
  761.9 24.8 %collective-permute-start = (bf16[256,1536]{1,0:T(8,128)(2,1)S(1)}, bf16[256,1536]{1,0:T(8,128)(2,1)}, u32[]{:S(2)}, u32[]{:S(2)}) collective-permute-start(bf16[256,1536]{1,0:T(8,128)(2,1)S(1)} %get-tuple-element.645), channel_id=1, source_target_pairs={{112,0},{0,16},{16,32},{32,48},{48,64},{64,80},{80,96},{96,112},{1... | collective-permute-start | bytes 2359304 | tf_op jit(solution)/shard_map/while/body/eval_jaxpr/ppermute | solution.py:12
  788.9 6.7 collective-permute-done
  797.1 7.9 collective-permute-start
  807.2 57.5 %collective-permute-done = bf16[256,1536]{1,0:T(8,128)(2,1)} collective-permute-done((bf16[256,1536]{1,0:T(8,128)(2,1)S(1)}, bf16[256,1536]{1,0:T(8,128)(2,1)}, u32[]{:S(2)}, u32[]{:S(2)}) %collective-permute-start) | collective-permute-done | bytes 786464 | tf_op jit(solution)/shard_map/while/body/eval_jaxpr/ppermute | solution.py:12
  868.6 40.2 %collective-permute-done = bf16[256,1536]{1,0:T(8,128)(2,1)} collective-permute-done((bf16[256,1536]{1,0:T(8,128)(2,1)S(1)}, bf16[256,1536]{1,0:T(8,128)(2,1)}, u32[]{:S(2)}, u32[]{:S(2)}) %collective-permute-start) | collective-permute-done | bytes 786464 | tf_op jit(solution)/shard_map/while/body/eval_jaxpr/ppermute | solution.py:12
  912.6 40.5 %collective-permute-done = bf16[256,1536]{1,0:T(8,128)(2,1)} collective-permute-done((bf16[256,1536]{1,0:T(8,128)(2,1)S(1)}, bf16[256,1536]{1,0:T(8,128)(2,1)}, u32[]{:S(2)}, u32[]{:S(2)}) %collective-permute-start) | collective-permute-done | bytes 786464 | tf_op jit(solution)/shard_map/while/body/eval_jaxpr/ppermute | solution.py:12
  965.9 110.0 %all-reduce.4.cloned.1.call-done = bf16[4,256,1536]{2,1,0:T(8,128)(2,1)} async-done(((bf16[4,256,1536]{2,1,0:T(8,128)(2,1)}), bf16[4,256,1536]{2,1,0:T(8,128)(2,1)}) %all-reduce.4.cloned.1.call-update) | async-done | bytes 3145744 | tf_op jit(solution)/shard_map/psum | solution.py:17
  1078.4 11.8 %while.30 = (s32[]{:T(128)}, f32[4,32]{1,0:T(4,128)S(1)}, bf16[4,32,768]{2,1,0:T(8,128)(2,1)S(1)}, bf16[4,256,768]{2,1,0:T(8,128)(2,1)}, s32[4,32,100]{1,2,0:T(8,128)S(1)}, /*index=5*/s32[]{:T(128)}, s32[]{:T(128)}, s32[]{:T(128)}) while((s32[]{:T(128)}, f32[4,32]{1,0:T(4,128)S(1)}, ...), condition=%wide.region_18.19_spmd.clone.clone, body=%wide.region_14.18_spmd.clone.clone.sunk | while | flops 15068354 | bytes 600169 | solution.py:59
  (186 shorter events, 151.9 us)
Async XLA Ops:
  6.5 953.2 %copy-start = (bf16[1536,768]{1,0:T(8,128)(2,1)S(1)}, bf16[1536,768]{1,0:T(8,128)(2,1)}, u32[]{:S(2)}) copy-start(bf16[1536,768]{1,0:T(8,128)(2,1)} %param.21) | copy-start | bytes 7077892
  6.5 128.6 %all-gather.4.cloned.1.call-start = ((), (), s32[]{:S(2)}) async-start(), calls=%async_computation.1 | async-start | bytes 20054016 | tf_op jit(solution)/shard_map/all_gather | solution.py:108
  6.5 36.5 %copy-start.3 = (bf16[1536]{0:T(1024)(128)(2,1)S(1)}, bf16[1536]{0:T(1024)(128)(2,1)}, u32[]{:S(2)}) copy-start(bf16[1536]{0:T(1024)(128)(2,1)} %param.19) | copy-start | bytes 9220
  7.3 1068.6 %all-reduce.4.cloned.1.call-start = ((), (), s32[]{:S(2)}) async-start(), calls=%async_computation | async-start | bytes 6291456 | tf_op jit(solution)/shard_map/psum | solution.py:17
  42.3 4.6 copy-start.1
  168.8 21.2 %collective-permute-start = (bf16[256,1536]{1,0:T(8,128)(2,1)S(1)}, bf16[256,1536]{1,0:T(8,128)(2,1)}, u32[]{:S(2)}, u32[]{:S(2)}) collective-permute-start(bf16[256,1536]{1,0:T(8,128)(2,1)S(1)} %get-tuple-element.645), channel_id=1, source_target_pairs={{112,0},{0,16},{16,32},{32,48},{48,64},{64,80},{80,96},{96,112},{1... | collective-permute-start | bytes 2359304 | tf_op jit(solution)/shard_map/while/body/eval_jaxpr/ppermute | solution.py:12
  220.9 20.3 %collective-permute-start = (bf16[256,1536]{1,0:T(8,128)(2,1)S(1)}, bf16[256,1536]{1,0:T(8,128)(2,1)}, u32[]{:S(2)}, u32[]{:S(2)}) collective-permute-start(bf16[256,1536]{1,0:T(8,128)(2,1)S(1)} %get-tuple-element.645), channel_id=1, source_target_pairs={{112,0},{0,16},{16,32},{32,48},{48,64},{64,80},{80,96},{96,112},{1... | collective-permute-start | bytes 2359304 | tf_op jit(solution)/shard_map/while/body/eval_jaxpr/ppermute | solution.py:12
  272.1 19.3 %collective-permute-start = (bf16[256,1536]{1,0:T(8,128)(2,1)S(1)}, bf16[256,1536]{1,0:T(8,128)(2,1)}, u32[]{:S(2)}, u32[]{:S(2)}) collective-permute-start(bf16[256,1536]{1,0:T(8,128)(2,1)S(1)} %get-tuple-element.645), channel_id=1, source_target_pairs={{112,0},{0,16},{16,32},{32,48},{48,64},{64,80},{80,96},{96,112},{1... | collective-permute-start | bytes 2359304 | tf_op jit(solution)/shard_map/while/body/eval_jaxpr/ppermute | solution.py:12
  322.4 18.4 %collective-permute-start = (bf16[256,1536]{1,0:T(8,128)(2,1)S(1)}, bf16[256,1536]{1,0:T(8,128)(2,1)}, u32[]{:S(2)}, u32[]{:S(2)}) collective-permute-start(bf16[256,1536]{1,0:T(8,128)(2,1)S(1)} %get-tuple-element.645), channel_id=1, source_target_pairs={{112,0},{0,16},{16,32},{32,48},{48,64},{64,80},{80,96},{96,112},{1... | collective-permute-start | bytes 2359304 | tf_op jit(solution)/shard_map/while/body/eval_jaxpr/ppermute | solution.py:12
  342.0 41.4 %collective-permute-start = (bf16[256,1536]{1,0:T(8,128)(2,1)S(1)}, bf16[256,1536]{1,0:T(8,128)(2,1)}, u32[]{:S(2)}, u32[]{:S(2)}) collective-permute-start(bf16[256,1536]{1,0:T(8,128)(2,1)S(1)} %get-tuple-element.645), channel_id=1, source_target_pairs={{112,0},{0,16},{16,32},{32,48},{48,64},{64,80},{80,96},{96,112},{1... | collective-permute-start | bytes 2359304 | tf_op jit(solution)/shard_map/while/body/eval_jaxpr/ppermute | solution.py:12
  384.7 16.9 %collective-permute-start = (bf16[256,1536]{1,0:T(8,128)(2,1)S(1)}, bf16[256,1536]{1,0:T(8,128)(2,1)}, u32[]{:S(2)}, u32[]{:S(2)}) collective-permute-start(bf16[256,1536]{1,0:T(8,128)(2,1)S(1)} %get-tuple-element.645), channel_id=1, source_target_pairs={{112,0},{0,16},{16,32},{32,48},{48,64},{64,80},{80,96},{96,112},{1... | collective-permute-start | bytes 2359304 | tf_op jit(solution)/shard_map/while/body/eval_jaxpr/ppermute | solution.py:12
  402.8 40.1 %collective-permute-start = (bf16[256,1536]{1,0:T(8,128)(2,1)S(1)}, bf16[256,1536]{1,0:T(8,128)(2,1)}, u32[]{:S(2)}, u32[]{:S(2)}) collective-permute-start(bf16[256,1536]{1,0:T(8,128)(2,1)S(1)} %get-tuple-element.645), channel_id=1, source_target_pairs={{112,0},{0,16},{16,32},{32,48},{48,64},{64,80},{80,96},{96,112},{1... | collective-permute-start | bytes 2359304 | tf_op jit(solution)/shard_map/while/body/eval_jaxpr/ppermute | solution.py:12
  444.1 76.7 %collective-permute-start = (bf16[256,1536]{1,0:T(8,128)(2,1)S(1)}, bf16[256,1536]{1,0:T(8,128)(2,1)}, u32[]{:S(2)}, u32[]{:S(2)}) collective-permute-start(bf16[256,1536]{1,0:T(8,128)(2,1)S(1)} %get-tuple-element.645), channel_id=1, source_target_pairs={{112,0},{0,16},{16,32},{32,48},{48,64},{64,80},{80,96},{96,112},{1... | collective-permute-start | bytes 2359304 | tf_op jit(solution)/shard_map/while/body/eval_jaxpr/ppermute | solution.py:12
  552.0 16.2 %collective-permute-start = (bf16[256,1536]{1,0:T(8,128)(2,1)S(1)}, bf16[256,1536]{1,0:T(8,128)(2,1)}, u32[]{:S(2)}, u32[]{:S(2)}) collective-permute-start(bf16[256,1536]{1,0:T(8,128)(2,1)S(1)} %get-tuple-element.645), channel_id=1, source_target_pairs={{112,0},{0,16},{16,32},{32,48},{48,64},{64,80},{80,96},{96,112},{1... | collective-permute-start | bytes 2359304 | tf_op jit(solution)/shard_map/while/body/eval_jaxpr/ppermute | solution.py:12
  599.3 15.2 %collective-permute-start = (bf16[256,1536]{1,0:T(8,128)(2,1)S(1)}, bf16[256,1536]{1,0:T(8,128)(2,1)}, u32[]{:S(2)}, u32[]{:S(2)}) collective-permute-start(bf16[256,1536]{1,0:T(8,128)(2,1)S(1)} %get-tuple-element.645), channel_id=1, source_target_pairs={{112,0},{0,16},{16,32},{32,48},{48,64},{64,80},{80,96},{96,112},{1... | collective-permute-start | bytes 2359304 | tf_op jit(solution)/shard_map/while/body/eval_jaxpr/ppermute | solution.py:12
  645.8 14.3 %collective-permute-start = (bf16[256,1536]{1,0:T(8,128)(2,1)S(1)}, bf16[256,1536]{1,0:T(8,128)(2,1)}, u32[]{:S(2)}, u32[]{:S(2)}) collective-permute-start(bf16[256,1536]{1,0:T(8,128)(2,1)S(1)} %get-tuple-element.645), channel_id=1, source_target_pairs={{112,0},{0,16},{16,32},{32,48},{48,64},{64,80},{80,96},{96,112},{1... | collective-permute-start | bytes 2359304 | tf_op jit(solution)/shard_map/while/body/eval_jaxpr/ppermute | solution.py:12
  691.2 13.1 %collective-permute-start = (bf16[256,1536]{1,0:T(8,128)(2,1)S(1)}, bf16[256,1536]{1,0:T(8,128)(2,1)}, u32[]{:S(2)}, u32[]{:S(2)}) collective-permute-start(bf16[256,1536]{1,0:T(8,128)(2,1)S(1)} %get-tuple-element.645), channel_id=1, source_target_pairs={{112,0},{0,16},{16,32},{32,48},{48,64},{64,80},{80,96},{96,112},{1... | collective-permute-start | bytes 2359304 | tf_op jit(solution)/shard_map/while/body/eval_jaxpr/ppermute | solution.py:12
  705.8 37.1 %collective-permute-start = (bf16[256,1536]{1,0:T(8,128)(2,1)S(1)}, bf16[256,1536]{1,0:T(8,128)(2,1)}, u32[]{:S(2)}, u32[]{:S(2)}) collective-permute-start(bf16[256,1536]{1,0:T(8,128)(2,1)S(1)} %get-tuple-element.645), channel_id=1, source_target_pairs={{112,0},{0,16},{16,32},{32,48},{48,64},{64,80},{80,96},{96,112},{1... | collective-permute-start | bytes 2359304 | tf_op jit(solution)/shard_map/while/body/eval_jaxpr/ppermute | solution.py:12
  744.4 16.0 %collective-permute-start = (bf16[256,1536]{1,0:T(8,128)(2,1)S(1)}, bf16[256,1536]{1,0:T(8,128)(2,1)}, u32[]{:S(2)}, u32[]{:S(2)}) collective-permute-start(bf16[256,1536]{1,0:T(8,128)(2,1)S(1)} %get-tuple-element.645), channel_id=1, source_target_pairs={{112,0},{0,16},{16,32},{32,48},{48,64},{64,80},{80,96},{96,112},{1... | collective-permute-start | bytes 2359304 | tf_op jit(solution)/shard_map/while/body/eval_jaxpr/ppermute | solution.py:12
  761.9 33.7 %collective-permute-start = (bf16[256,1536]{1,0:T(8,128)(2,1)S(1)}, bf16[256,1536]{1,0:T(8,128)(2,1)}, u32[]{:S(2)}, u32[]{:S(2)}) collective-permute-start(bf16[256,1536]{1,0:T(8,128)(2,1)S(1)} %get-tuple-element.645), channel_id=1, source_target_pairs={{112,0},{0,16},{16,32},{32,48},{48,64},{64,80},{80,96},{96,112},{1... | collective-permute-start | bytes 2359304 | tf_op jit(solution)/shard_map/while/body/eval_jaxpr/ppermute | solution.py:12
  797.1 67.6 %collective-permute-start = (bf16[256,1536]{1,0:T(8,128)(2,1)S(1)}, bf16[256,1536]{1,0:T(8,128)(2,1)}, u32[]{:S(2)}, u32[]{:S(2)}) collective-permute-start(bf16[256,1536]{1,0:T(8,128)(2,1)S(1)} %get-tuple-element.645), channel_id=1, source_target_pairs={{112,0},{0,16},{16,32},{32,48},{48,64},{64,80},{80,96},{96,112},{1... | collective-permute-start | bytes 2359304 | tf_op jit(solution)/shard_map/while/body/eval_jaxpr/ppermute | solution.py:12
  866.2 42.5 %collective-permute-start = (bf16[256,1536]{1,0:T(8,128)(2,1)S(1)}, bf16[256,1536]{1,0:T(8,128)(2,1)}, u32[]{:S(2)}, u32[]{:S(2)}) collective-permute-start(bf16[256,1536]{1,0:T(8,128)(2,1)S(1)} %get-tuple-element.645), channel_id=1, source_target_pairs={{112,0},{0,16},{16,32},{32,48},{48,64},{64,80},{80,96},{96,112},{1... | collective-permute-start | bytes 2359304 | tf_op jit(solution)/shard_map/while/body/eval_jaxpr/ppermute | solution.py:12
  910.2 42.8 %collective-permute-start = (bf16[256,1536]{1,0:T(8,128)(2,1)S(1)}, bf16[256,1536]{1,0:T(8,128)(2,1)}, u32[]{:S(2)}, u32[]{:S(2)}) collective-permute-start(bf16[256,1536]{1,0:T(8,128)(2,1)S(1)} %get-tuple-element.645), channel_id=1, source_target_pairs={{112,0},{0,16},{16,32},{32,48},{48,64},{64,80},{80,96},{96,112},{1... | collective-permute-start | bytes 2359304 | tf_op jit(solution)/shard_map/while/body/eval_jaxpr/ppermute | solution.py:12
  958.8 0.8 copy-start.2
  1090.2 0.6 copy-start.4
Sparse Core Ops, SparseCore 0:
  9.8 125.2 all-gather.3
  958.9 116.8 all-reduce.3
where the time goes:
time: 1100 us
  waiting for transfers between devices  585 us (53%)
  other arithmetic  277 us (25%)
  starting transfers between devices  127 us (12%)
  matrix products  54.7 us (5%)
  blocking collectives  32.6 us (3%)
  between operations  13.5 us (1%)
    ppermute x18, waiting for transfers between devices, passed_along(): return lax.ppermute(block, axis, route)  386 us
    convert_element_type x8, other arithmetic, conv_module(): return (values + jax.nn.silu(mixed)).astype(jnp.bfloat16)  175 us
    ppermute x18, starting transfers between devices, passed_along(): return lax.ppermute(block, axis, route)  127 us
    psum x1, waiting for transfers between devices, spread_2(): return lax.psum(kept, axis)  110 us
    all_gather x1, waiting for transfers between devices, on_device(): lax.all_gather(weight_rows, 'fsdp', axis=1, tiled=True)  88.1 us
    dot_general x8, matrix products, conv_module(): proj = jnp.dot(normed, weight, preferred_element_type=jnp.float32)  42.1 us
    select_n x19, other arithmetic, advance(): finished = jnp.where(write, updated, finished)  42.1 us
    all_gather x1, blocking collectives, on_device(): lax.all_gather(kernel_cols, 'fsdp', axis=2, tiled=True)  32.6 us
  transfers between devices with their start and end apart: 20, of which 20 were waited for; matrix products, arithmetic and copies ran while one was open for 5% of the time, Pallas kernels for 0%

commit v1 on v0

v1 whole, which is shorter than its diff:
```python
import functools

import jax
import jax.numpy as jnp
from jax import lax
from jax.experimental import pallas as pl
from jax.experimental.pallas import tpu as pltpu
from jax.sharding import PartitionSpec as P

MASK_LEN = 10
TAPS = 31
CW = 256
LANES = 128
PAD = 16
GROUP = 64
MESH = pl.DeviceIdType.MESH


def relay_kernel(
    sections,
    x0_hbm,
    w_hbm,
    wctx_ref,
    tgt_ref,
    cnt_ref,
    out_ref,
    xin,
    xmid,
    obuf,
    nrm,
    gbuf,
    wv,
    kv,
    enc,
    cbuf,
    w_sem,
    x_sem,
    send_sem,
    recv_sem,
    csend_sem,
    crecv_sem,
):
    micro, chunks, frames, _ = xin.shape
    width = chunks * CW
    share = frames // sections
    s = lax.axis_index("section")
    last = sections - 1
    nxt = lax.rem(s + 1, sections)
    barrier = pltpu.get_barrier_semaphore()
    for j in range(sections):

        @pl.when(s != j)
        def _():
            pl.semaphore_signal(barrier, inc=1, device_id={"section": j}, device_id_type=MESH)

    pl.semaphore_wait(barrier, sections - 1)

    def load_w(layer):
        return pltpu.make_async_copy(w_hbm.at[layer], wv.at[layer], w_sem.at[layer])

    def load_x():
        return pltpu.make_async_copy(x0_hbm, xin, x_sem)

    load_w(0).start()

    @pl.when(s == 0)
    def _():
        load_x().start()

    load_w(1).start()

    for b in range(2):
        gbuf[b, 0:PAD, :] = jnp.zeros((PAD, LANES), jnp.float32)
        gbuf[b, PAD + frames : 2 * PAD + frames, :] = jnp.zeros((PAD, LANES), jnp.float32)

    def hop(i, c):
        return pltpu.make_async_remote_copy(
            src_ref=obuf.at[i, c],
            dst_ref=xin.at[i, c],
            send_sem=send_sem.at[i, c],
            recv_sem=recv_sem.at[i, c],
            device_id={"section": nxt},
            device_id_type=MESH,
        )

    def scatter(i, j):
        return pltpu.make_async_remote_copy(
            src_ref=cbuf.at[i, pl.ds(j * share, share)],
            dst_ref=enc.at[i],
            send_sem=csend_sem.at[i, j],
            recv_sem=crecv_sem.at[i],
            device_id={"section": j},
            device_id_type=MESH,
        )

    def taps_of(layer):
        for h in range(width // LANES):
            block = wv[layer, h * LANES : (h + 1) * LANES, 2 * width : 2 * width + LANES]
            kv[layer, h] = block.astype(jnp.float32).T[0:32, :]

    def normalise(x):
        total = jnp.zeros((frames, 1), jnp.float32)
        for c in range(chunks):
            total = total + jnp.sum(x[c].astype(jnp.float32), axis=1, keepdims=True)
        center = total / width
        total = jnp.zeros((frames, 1), jnp.float32)
        for c in range(chunks):
            off = x[c].astype(jnp.float32) - center
            total = total + jnp.sum(off * off, axis=1, keepdims=True)
        scale = lax.rsqrt(total / width + 1e-05)
        for c in range(chunks):
            off = x[c].astype(jnp.float32) - center
            nrm[:, c * CW : (c + 1) * CW] = (off * scale).astype(jnp.bfloat16)

    def chunk(layer, x, y, c):
        col = pl.multiple_of(c * CW, CW)
        gate_col = pl.multiple_of(width + c * CW, CW)
        value = jnp.dot(
            nrm[...], wv[layer, :, pl.ds(col, CW)], preferred_element_type=jnp.float32
        )
        gate = jnp.dot(
            nrm[...], wv[layer, :, pl.ds(gate_col, CW)], preferred_element_type=jnp.float32
        )
        glu = (value * jax.nn.sigmoid(gate)).astype(jnp.bfloat16).astype(jnp.float32)
        for h in range(CW // LANES):
            gbuf[h, PAD : PAD + frames, :] = glu[:, h * LANES : (h + 1) * LANES]
        for h in range(CW // LANES):
            for r in range(0, frames, GROUP):
                mixed = jnp.zeros((GROUP, LANES), jnp.float32)
                for k in range(TAPS):
                    taps = kv[layer, c * (CW // LANES) + h, k : k + 1, :]
                    mixed = mixed + gbuf[h, r + k + 1 : r + k + 1 + GROUP, :] * taps
                kept = x[c, r : r + GROUP, h * LANES : (h + 1) * LANES].astype(jnp.float32)
                y[c, r : r + GROUP, h * LANES : (h + 1) * LANES] = (
                    kept + mixed * jax.nn.sigmoid(mixed)
                ).astype(jnp.bfloat16)

    def one_micro(i, carry):
        @pl.when((i == 0) & (s == 0))
        def _():
            load_x().wait()

        @pl.when(s > 0)
        def _():
            for c in range(chunks):
                hop(i, c).wait_recv()

        normalise(xin.at[i])

        @pl.when(i == 0)
        def _():
            load_w(0).wait()
            taps_of(0)

        def chunk_a(c, carry):
            chunk(0, xin.at[i], xmid, c)
            return carry

        lax.fori_loop(0, chunks, chunk_a, 0)
        normalise(xmid)

        @pl.when(i == 0)
        def _():
            load_w(1).wait()
            taps_of(1)

        def chunk_b(c, carry):
            chunk(1, xmid, obuf.at[i], c)

            @pl.when(s < last)
            def _():
                hop(i, c).start()

            return carry

        lax.fori_loop(0, chunks, chunk_b, 0)

        @pl.when(s == last)
        def _():
            ctx = jnp.zeros((frames, wctx_ref.shape[1]), jnp.float32)
            for c in range(chunks):
                ctx = ctx + jnp.dot(
                    obuf[i, c],
                    wctx_ref[c * CW : (c + 1) * CW, :],
                    preferred_element_type=jnp.float32,
                )
            size = jnp.sum(ctx * ctx, axis=1, keepdims=True)
            cbuf[i] = (ctx * lax.rsqrt(size + 1e-06)).astype(jnp.bfloat16)
            for j in range(sections - 1):
                scatter(i, j).start()

        return carry

    lax.fori_loop(0, micro, one_micro, 0)

    @pl.when(s < last)
    def _():
        for i in range(micro):
            scatter(i, 0).wait_recv()

    @pl.when(s == last)
    def _():
        for i in range(micro):
            enc[i] = cbuf[i, last * share : (last + 1) * share, :]

    spots = lax.broadcasted_iota(jnp.int32, (share, frames), 1)
    rows = lax.broadcasted_iota(jnp.int32, (share, frames), 0) + s * share
    for i in range(micro):
        sims = 10.0 * lax.dot_general(
            enc[i], tgt_ref[i], (((1,), (1,)), ((), ())), preferred_element_type=jnp.float32
        )
        positive = jnp.sum(jnp.where(spots == rows, sims, 0.0), axis=1, keepdims=True)
        negative = jnp.sum(cnt_ref[i] * jnp.exp(sims), axis=1, keepdims=True)
        out_ref[i] = jnp.log(jnp.exp(positive) + negative) - positive

    @pl.when(s < last)
    def _():
        for i in range(micro):
            for c in range(chunks):
                hop(i, c).wait_send()

    @pl.when(s == last)
    def _():
        for i in range(micro):
            for j in range(sections - 1):
                scatter(i, j).wait_send()


def relay(sections, masked_in, weights, w_ctx, tgt, counts):
    micro, frames, width = masked_in.shape
    chunks = width // CW
    share = frames // sections
    proj = w_ctx.shape[1]
    x0 = masked_in.reshape(micro, frames, chunks, CW).transpose(0, 2, 1, 3)
    vmem = pl.BlockSpec(memory_space=pltpu.VMEM)
    hbm = pl.BlockSpec(memory_space=pl.ANY)
    return pl.pallas_call(
        functools.partial(relay_kernel, sections),
        out_shape=jax.ShapeDtypeStruct((micro, share, 1), jnp.float32),
        in_specs=[hbm, hbm, vmem, vmem, vmem],
        out_specs=vmem,
        scratch_shapes=[
            pltpu.VMEM((micro, chunks, frames, CW), jnp.bfloat16),
            pltpu.VMEM((chunks, frames, CW), jnp.bfloat16),
            pltpu.VMEM((micro, chunks, frames, CW), jnp.bfloat16),
            pltpu.VMEM((frames, width), jnp.bfloat16),
            pltpu.VMEM((CW // LANES, frames + 2 * PAD, LANES), jnp.float32),
            pltpu.VMEM(weights.shape, jnp.bfloat16),
            pltpu.VMEM((2, width // LANES, 32, LANES), jnp.float32),
            pltpu.VMEM((micro, share, proj), jnp.bfloat16),
            pltpu.VMEM((micro, frames, proj), jnp.bfloat16),
            pltpu.SemaphoreType.DMA((2,)),
            pltpu.SemaphoreType.DMA,
            pltpu.SemaphoreType.DMA((micro, chunks)),
            pltpu.SemaphoreType.DMA((micro, chunks)),
            pltpu.SemaphoreType.DMA((micro, sections)),
            pltpu.SemaphoreType.DMA((micro,)),
        ],
        compiler_params=pltpu.CompilerParams(
            collective_id=0, has_side_effects=True, vmem_limit_bytes=56 << 20
        ),
    )(x0, weights, w_ctx, tgt, counts)


def unit_rows(values):
    return (values * lax.rsqrt(jnp.sum(values * values, axis=-1, keepdims=True) + 1e-06)).astype(
        jnp.bfloat16
    )


def on_device(feats, w_in, dw_kernel, mask_embed, w_ctx, w_tgt, mask_starts, distractors):
    sections = lax.axis_size("section")
    section = lax.axis_index("section")
    frames = feats.shape[2]
    feats_local = feats[:, 0]
    half = sections // 2

    taps = dw_kernel[:, 0].transpose(0, 2, 1)
    taps = jnp.pad(taps, ((0, 0), (0, 0), (0, LANES - taps.shape[2])))
    rows = jnp.concatenate([w_in[:, 0], taps], axis=2)
    even = section % 2 == 0
    first = jnp.where(even, rows[0], rows[1])
    second = jnp.where(even, rows[1], rows[0])
    route_1 = [(i, i // 2 if i % 2 == 0 else half + i // 2) for i in range(sections)]
    route_2 = [(i, half + i // 2 if i % 2 == 0 else i // 2) for i in range(sections)]
    got_1 = lax.ppermute(first, "section", route_1)
    got_2 = lax.ppermute(second, "section", route_2)
    low = section < half
    pair = jnp.stack([jnp.where(low, got_1, got_2), jnp.where(low, got_2, got_1)])
    weights = lax.all_gather(pair, "fsdp", axis=1, tiled=True)

    spots = jnp.arange(frames, dtype=jnp.int32)
    starts = mask_starts[:, 0][:, :, None]
    covered = jnp.any(
        (spots[None, None, :] >= starts) & (spots[None, None, :] < starts + MASK_LEN), axis=1
    )
    masked_in = jnp.where(covered[:, :, None], mask_embed[None, None, :], feats_local)
    tgt = unit_rows(
        jnp.einsum("mjd,de->mje", feats_local, w_tgt, preferred_element_type=jnp.float32)
    )
    picks = distractors[:, 0]
    counts = jnp.sum((picks[..., None] == spots).astype(jnp.float32), axis=2)
    loss = relay(sections, masked_in, weights, w_ctx, tgt, counts)
    return loss[:, :, 0][:, None, :]


def solution(mesh):
    placed = (
        P(None, "fsdp", None, None),
        P(None, "section", "fsdp", None),
        P(None, "section", None, "fsdp"),
        P(),
        P(),
        P(),
        P(None, "fsdp", None),
        P(None, "fsdp", "section", None),
    )
    return jax.shard_map(
        on_device, mesh=mesh, in_specs=placed, out_specs=P(None, "fsdp", "section"), check_vma=False
    )
```

time: 1100 us -> 456 us (0.41)
  waiting for transfers between devices: 585 us -> 129 us
  Pallas kernels: 0 us -> 272 us
  other arithmetic: 277 us -> 13.5 us
  starting transfers between devices: 127 us -> 7.58 us
  matrix products: 54.7 us -> 4.71 us
  blocking collectives: 32.6 us -> 0 us
    ppermute x18 -> x2, waiting for transfers between devices: 386 us -> 12.5 us  [the longest x1 12.5 us: on_device(): got_2 = lax.ppermute(second, 'section', route_2)]
    pallas_call x0 -> x1, Pallas kernels: none -> 272 us  [relay(): pl.pallas_call(functools.partial(relay_kernel, sections), out_shape=jax.S...]
    convert_element_type x32 -> x0, other arithmetic: 191 us -> none  [the longest x8 175 us: conv_module(): return (values + jax.nn.silu(mixed)).astype(jnp.bfloat16)]
    ppermute x18 -> x2, starting transfers between devices: 127 us -> 7.58 us  [the longest x1 5.86 us: on_device(): got_2 = lax.ppermute(second, 'section', route_2)]
    psum x1 -> x0, waiting for transfers between devices: 110 us -> none  [spread_2(): return lax.psum(kept, axis)]
    select_n x40 -> x1, other arithmetic: 73.6 us -> 1.15 us  [on_device(): first = jnp.where(even, rows[0], rows[1])]
    dot_general x13 -> x0, matrix products: 49.9 us -> none  [the longest x8 42.1 us: conv_module(): proj = jnp.dot(normed, weight, preferred_element_type=jnp.float32)]
    all_gather x1 -> x0, blocking collectives: 32.6 us -> none  [on_device(): lax.all_gather(kernel_cols, 'fsdp', axis=2, tiled=True)]
  transfers between devices with their start and end apart: 20 -> 3, of which waited for: 20 -> 2; matrix products, arithmetic and copies ran while one was open for 5% -> 5% of each run, Pallas kernels for 0% -> 0%
where the time goes in v1:
time: 456 us; the launch traced here: 451 us
  Pallas kernels  272 us (60%)
  waiting for transfers between devices  129 us (28%)
  other arithmetic  13.5 us (3%)
  between operations  13.5 us (3%)
  local copies, waits for them, and re-layouts  10.8 us (2%)
  starting transfers between devices  7.58 us (2%)
  matrix products  4.71 us (1%)
    pallas_call x1, Pallas kernels, relay(): pl.pallas_call(functools.partial(relay_kernel, sections), out_shape=jax.S...  272 us
    all_gather x1, waiting for transfers between devices, on_device(): weights = lax.all_gather(pair, 'fsdp', axis=1, tiled=True)  116 us
    ppermute x1, waiting for transfers between devices, on_device(): got_2 = lax.ppermute(second, 'section', route_2)  12.5 us
  transfers between devices with their start and end apart: 3, of which 2 were waited for; matrix products, arithmetic and copies ran while one was open for 5% of the time, Pallas kernels for 0%

profile of v1, /device:TPU:1, one launch (start us, length us, event | category | flops | bytes accessed | tf_op | source)
XLA Modules:
  0.0 451.0 jit_solution(1675917651948086322)
XLA Ops:
  6.5 0.0 copy-start
  6.5 0.0 all-gather.2.cloned.1.call-start
  6.5 1.0 copy.19
  7.5 1.4 fusion.4
  8.9 1.1 select_bitcast_fusion.4
  10.0 1.7 collective-permute-start
  11.8 5.9 %collective-permute-start.1 = (bf16[96,3200]{1,0:T(8,128)(2,1)}, bf16[96,3200]{1,0:T(8,128)(2,1)}, u32[]{:S(2)}, u32[]{:S(2)}) collective-permute-start(bf16[96,3200]{1,0:T(8,128)(2,1)} %get-tuple-element.8), channel_id=1, source_target_pairs={{0,64},{16,0},{32,80},{48,16},{64,96},{80,32},{96,112},{112,48},{1... | collective-permute-start | bytes 1843208 | tf_op jit(solution)/shard_map/ppermute | solution.py:287
  17.6 0.0 collective-permute-done
  17.6 12.5 %collective-permute-done.1 = bf16[96,3200]{1,0:T(8,128)(2,1)} collective-permute-done((bf16[96,3200]{1,0:T(8,128)(2,1)}, bf16[96,3200]{1,0:T(8,128)(2,1)}, u32[]{:S(2)}, u32[]{:S(2)}) %collective-permute-start.1) | collective-permute-done | bytes 614432 | tf_op jit(solution)/shard_map/ppermute | solution.py:287
  30.1 1.2 select_bitcast_fusion.2
  31.3 0.0 copy-start.3
  31.3 1.2 pad_maximum_fusion
  32.5 0.0 all-gather.2.cloned.1.call-update
  32.5 0.0 copy-done.3
  32.5 0.1 copy.15
  32.6 0.1 copy.16
  32.7 4.7 %copy.17 = bf16[4,1,256,1536]{2,3,0,1:T(8,128)(2,1)} copy(bf16[4,1,256,1536]{3,2,1,0:T(8,128)(2,1)} %param.8) | data formatting | bytes 6291456 | tf_op args[0]
  37.4 0.0 copy-start.4
  37.4 0.0 copy-start.2
  37.4 4.7 %copy.18 = bf16[4,256,6,256]{3,1,2,0:T(8,128)(2,1)} copy(bf16[4,256,6,256]{1,3,2,0:T(8,128)(2,1)} %bitcast.30) | data formatting | bytes 6291456 | tf_op jit(solution)/shard_map/squeeze | solution.py:275
  42.1 0.0 copy-done.4
  42.2 0.0 copy-done.2
  42.2 0.1 copy.20
  42.3 0.1 fusion.6
  42.4 0.0 copy-done
  42.4 4.7 %multiply_reduce_fusion = (f32[4,256]{1,0:T(4,128)S(1)}, f32[4,256,768]{2,1,0:T(8,128)S(1)}) fusion(bf16[1536,768]{1,0:T(8,128)(2,1)S(1)} %copy-done, bf16[4,1,256,1536]{3,2,1,0:T(8,128)(2,1)} %param.8), kind=kOutput, calls=%fused_computation.5 | convolution fusion | flops 2417490944 | bytes 8654848 | tf_op jit(solution)/shard_map/mjd,de->mje/dot_general | solution.py:299
  47.1 0.0 copy-start.1
  47.1 3.6 convert_reduce_fusion.cnt_ref
  50.8 1.4 multiply_convert_fusion.tgt_ref
  52.2 0.0 copy-done.1
  52.2 2.0 select_bitcast_fusion.x0_hbm
  54.2 116.1 %all-gather.2.cloned.1.call-done.w_hbm = bf16[2,1536,3200]{2,1,0:T(8,128)(2,1)} async-done(((bf16[2,96,3200]{2,1,0:T(8,128)(2,1)}), bf16[2,1536,3200]{2,1,0:T(8,128)(2,1)}) %all-gather.2.cloned.1.call-update) | async-done | bytes 19660816 | tf_op jit(solution)/shard_map/all_gather | solution.py:290
  170.3 272.3 %shard_map.82 = f32[4,32,1]{2,1,0:T(8,128)} custom-call(bf16[4,6,256,256]{3,2,1,0:T(8,128)(2,1)} %select_bitcast_fusion.x0_hbm, bf16[2,1536,3200]{2,1,0:T(8,128)(2,1)} %all-gather.2.cloned.1.call-done.w_hbm, bf16[1536,768]{1,0:T(8,128)(2,1)} %wctx_ref.1, bf16[4,256,768]{2,1,0:T(8,128)(2,1)} %multiply_convert_fusion.tgt_ref, ...), custom_call_target="tpu_custom_call" | custom-call | tf_op jit(solution)/shard_map/pallas_call | solution.py:237
  442.6 1.5 reduce
  (3 shorter events, 0.0 us)
Async XLA Ops:
  6.5 35.9 %copy-start = (bf16[1536,768]{1,0:T(8,128)(2,1)S(1)}, bf16[1536,768]{1,0:T(8,128)(2,1)}, u32[]{:S(2)}) copy-start(bf16[1536,768]{1,0:T(8,128)(2,1)} %param.13) | copy-start | bytes 7077892
  6.5 163.8 %all-gather.2.cloned.1.call-start = ((), (), s32[]{:S(2)}) async-start(), calls=%async_computation | async-start | bytes 20889600 | tf_op jit(solution)/shard_map/all_gather | solution.py:290
  10.0 7.6 %collective-permute-start = (bf16[96,3200]{1,0:T(8,128)(2,1)}, bf16[96,3200]{1,0:T(8,128)(2,1)S(1)}, u32[]{:S(2)}, u32[]{:S(2)}) collective-permute-start(bf16[96,3200]{1,0:T(8,128)(2,1)} %get-tuple-element.7), channel_id=1, source_target_pairs={{0,0},{16,64},{32,16},{48,80},{64,32},{80,96},{96,48},{112,112},{1... | collective-permute-start | bytes 1843208 | tf_op jit(solution)/shard_map/ppermute | solution.py:286
  11.8 18.4 %collective-permute-start.1 = (bf16[96,3200]{1,0:T(8,128)(2,1)}, bf16[96,3200]{1,0:T(8,128)(2,1)}, u32[]{:S(2)}, u32[]{:S(2)}) collective-permute-start(bf16[96,3200]{1,0:T(8,128)(2,1)} %get-tuple-element.8), channel_id=1, source_target_pairs={{0,64},{16,0},{32,80},{48,16},{64,96},{80,32},{96,112},{112,48},{1... | collective-permute-start | bytes 1843208 | tf_op jit(solution)/shard_map/ppermute | solution.py:287
  31.3 1.2 copy-start.3
  37.4 4.7 %copy-start.4 = (bf16[1536]{0:T(1024)(128)(2,1)S(1)}, bf16[1536]{0:T(1024)(128)(2,1)}, u32[]{:S(2)}) copy-start(bf16[1536]{0:T(1024)(128)(2,1)} %param.11) | copy-start | bytes 9220
  37.4 4.7 %copy-start.2 = (s32[4,1,32,100]{3,2,1,0:T(8,128)S(1)}, s32[4,1,32,100]{3,2,1,0:T(8,128)}, u32[]{:S(2)}) copy-start(s32[4,1,32,100]{3,2,1,0:T(8,128)} %param.15) | copy-start | bytes 153604
  47.1 5.0 %copy-start.1 = (bf16[4,256,6,256]{3,1,2,0:T(8,128)(2,1)S(1)}, bf16[4,256,6,256]{3,1,2,0:T(8,128)(2,1)}, u32[]{:S(2)}) copy-start(bf16[4,256,6,256]{3,1,2,0:T(8,128)(2,1)} %copy.18) | copy-start | bytes 9437188
Sparse Core Ops, SparseCore 0:
  32.6 137.6 all-gather.1

commit v2 on v1

v2 whole, which is shorter than its diff:
```python
import functools

import jax
import jax.numpy as jnp
from jax import lax
from jax.experimental import pallas as pl
from jax.experimental.pallas import tpu as pltpu
from jax.sharding import PartitionSpec as P

MASK_LEN = 10
TAPS = 31
CW = 256
LANES = 128
PAD = 16
GROUP = 64
CORES = 2
MESH = pl.DeviceIdType.MESH


def relay_kernel(
    sections,
    columns,
    feats_ref,
    wcat_ref,
    wctx_ref,
    wtgt_ref,
    embed_ref,
    starts_ref,
    picks_ref,
    out_ref,
    xin,
    xmid,
    obuf,
    pbuf,
    nrm,
    gbuf,
    wv,
    kv,
    tgt,
    cnt,
    enc,
    cbuf,
    own_send,
    own_recv,
    ring_send,
    ring_recv,
    init_send,
    init_recv,
    hop_send,
    hop_recv,
    fwd_send,
    fwd_recv,
    mid_send,
    mid_recv,
    fin_send,
    fin_recv,
    csend_sem,
    crecv_sem,
):
    utts, chunks, frames, _ = xin.shape
    micro = utts // CORES
    mine = chunks // CORES
    width = chunks * CW
    half = width // CORES
    share = frames // sections
    last = sections - 1
    rows = width // columns
    piece = rows * CORES
    s = lax.axis_index("section")
    f = lax.axis_index("fsdp")
    core = lax.rem(f, 2)
    peer = f + 1 - 2 * core
    x_hi = lax.rem(f // 2, 2)
    across = f + 2 - 4 * x_hi
    y = f // 4
    ys = columns // 4
    up = lax.rem(f + 4, columns)
    down = lax.rem(f + columns - 4, columns)
    nxt = lax.rem(s + 1, sections)

    barrier = pltpu.get_barrier_semaphore()
    for j in range(sections):

        @pl.when(s != j)
        def _():
            pl.semaphore_signal(
                barrier, inc=1, device_id={"section": j, "fsdp": f}, device_id_type=MESH
            )

        pl.semaphore_signal(
            barrier, inc=1, device_id={"section": j, "fsdp": peer}, device_id_type=MESH
        )
    for g in (up, down, across):
        pl.semaphore_signal(barrier, inc=1, device_id={"section": s, "fsdp": g}, device_id_type=MESH)
    pl.semaphore_wait(barrier, 2 * sections - 1 + 3)

    def remote(src, dst, send, recv, section, column):
        return pltpu.make_async_remote_copy(
            src_ref=src,
            dst_ref=dst,
            send_sem=send,
            recv_sem=recv,
            device_id={"section": section, "fsdp": column},
            device_id_type=MESH,
        )

    def rows_of(column):
        return pl.ds(pl.multiple_of(column * rows, 32), rows)

    def own_out(t, h):
        return remote(
            wcat_ref.at[t, h],
            wv.at[lax.rem(s, 2), rows_of(f)],
            own_send.at[t, h],
            own_recv.at[lax.rem(s, 2), core],
            s // 2 + (sections // 2) * t,
            f - core + h,
        )

    def own_here(t, h):
        return pltpu.make_async_copy(
            wcat_ref.at[t, h],
            wv.at[lax.rem(s, 2), rows_of(f)],
            own_recv.at[lax.rem(s, 2), core],
        )

    def own_in(a, c):
        return remote(
            wcat_ref.at[0, 0],
            wv.at[a, rows_of(f - core + c)],
            own_send.at[0, 0],
            own_recv.at[a, c],
            s,
            peer,
        )

    stays = [(s == 0), (s == last)]
    for t in range(2):
        for h in range(CORES):
            here = stays[t] & (core == h)

            @pl.when(here)
            def _():
                own_here(t, h).start()

            @pl.when(jnp.logical_not(here))
            def _():
                own_out(t, h).start()

    def part(y_at, x_at):
        chip = lax.rem(y_at + 2 * ys, ys) * 2 + x_at
        return pl.ds(pl.multiple_of(chip * piece, 64), piece)

    def ring(a, n, y_at, x_at, column):
        block = wv.at[a, part(y_at, x_at)]
        return remote(block, block, ring_send.at[a, n], ring_recv.at[a, n], s, column)

    other = 1 - x_hi

    def ring_out(a, n):
        y_at, x_at, column = (
            (y, x_hi, across),
            (y, x_hi, up),
            (y, x_hi, down),
            (y, other, up),
            (y, other, down),
            (y - 1, x_hi, up),
            (y + 1, other, down),
        )[n]
        return ring(a, n, y_at, x_at, column)

    def ring_in(a, n):
        y_at, x_at, column = (
            (y, other, across),
            (y - 1, x_hi, up),
            (y + 1, x_hi, down),
            (y - 1, other, up),
            (y + 1, other, down),
            (y - 2, x_hi, up),
            (y + 2, other, down),
        )[n]
        return ring(a, n, y_at, x_at, column)

    def gather_1(a):
        for c in range(CORES):
            t = a
            here = stays[t] & (core == c)

            @pl.when(here)
            def _():
                own_here(t, c).wait()

            @pl.when(jnp.logical_not(here))
            def _():
                own_in(a, c).wait_recv()

        for n in (0, 1, 2):
            ring_out(a, n).start()

    def gather_2(a):
        ring_in(a, 0).wait_recv()
        ring_out(a, 3).start()
        ring_out(a, 4).start()
        ring_in(a, 1).wait_recv()
        ring_out(a, 5).start()
        ring_in(a, 4).wait_recv()
        ring_out(a, 6).start()

    def gather_3(a):
        for n in (2, 3, 5, 6):
            ring_in(a, n).wait_recv()

    def init(m):
        at = xin.at[CORES * m + core]
        return remote(at, at, init_send.at[m], init_recv.at[m], s, peer)

    def init_in(m):
        at = xin.at[CORES * m + 1 - core]
        return remote(at, at, init_send.at[m], init_recv.at[m], s, peer)

    gather_1(0)

    @pl.when(s == 0)
    def _():
        spot = lax.broadcasted_iota(jnp.int32, (frames, CW), 0)

        def one(m, carry):
            covered = jnp.zeros((frames, CW), jnp.int32)
            for j in range(starts_ref.shape[1]):
                start = starts_ref[m, j]
                inside = (spot >= start) & (spot < start + MASK_LEN)
                covered = jnp.where(inside, 1, covered)
            for c in range(chunks):
                embed = embed_ref[:, c * CW : (c + 1) * CW].astype(jnp.float32)
                seen = feats_ref[m, :, c * CW : (c + 1) * CW].astype(jnp.float32)
                xin[CORES * m + core, c] = jnp.where(covered > 0, embed, seen).astype(jnp.bfloat16)
            init(m).start()
            return carry

        lax.fori_loop(0, micro, one, 0)

    def targets(m, carry):
        proj = jnp.dot(feats_ref[m], wtgt_ref[...], preferred_element_type=jnp.float32)
        size = jnp.sum(proj * proj, axis=1, keepdims=True)
        tgt[m] = (proj * lax.rsqrt(size + 1e-06)).astype(jnp.bfloat16)
        spots = lax.broadcasted_iota(jnp.int32, (share, frames), 1)
        total = jnp.zeros((share, frames), jnp.float32)
        for k in range(picks_ref.shape[2]):
            total = total + jnp.where(picks_ref[m, :, k : k + 1] == spots, 1.0, 0.0)
        cnt[m] = total
        return carry

    gather_2(0)
    gather_1(1)
    lax.fori_loop(0, micro, targets, 0)

    for b in range(CW // LANES):
        gbuf[b, 0:PAD, :] = jnp.zeros((PAD, LANES), jnp.float32)
        gbuf[b, PAD + frames : 2 * PAD + frames, :] = jnp.zeros((PAD, LANES), jnp.float32)

    gather_2(1)
    gather_3(0)

    def taps_of(a):
        for h in range(half // LANES):
            at = pl.ds(pl.multiple_of(core * half + h * LANES, LANES), LANES)
            block = wv[a, at, 2 * half : 2 * half + LANES]
            kv[a, h] = block.astype(jnp.float32).T[0:32, :]

    taps_of(0)

    def hop(i, j):
        return remote(
            obuf.at[i, j],
            xin.at[i, core * mine + j],
            hop_send.at[i, j],
            hop_recv.at[i, j],
            nxt,
            f,
        )

    def forward(i, j):
        at = xin.at[i, core * mine + j]
        return remote(at, at, fwd_send.at[i, j], fwd_recv.at[i, j], s, peer)

    def forward_in(i, j):
        at = xin.at[i, (1 - core) * mine + j]
        return remote(at, at, fwd_send.at[i, j], fwd_recv.at[i, j], s, peer)

    def middle(i, j):
        at = xmid.at[i, core * mine + j]
        return remote(at, at, mid_send.at[i, j], mid_recv.at[i, j], s, peer)

    def middle_in(i, j):
        at = xmid.at[i, (1 - core) * mine + j]
        return remote(at, at, mid_send.at[i, j], mid_recv.at[i, j], s, peer)

    def final(i, j):
        m = i // CORES
        return remote(obuf.at[i, j], pbuf.at[m, j], fin_send.at[m, j], fin_recv.at[m, j], s, peer)

    def scatter(m, j):
        return remote(
            cbuf.at[m, pl.ds(j * share, share)],
            enc.at[m],
            csend_sem.at[m, j],
            crecv_sem.at[m],
            j,
            f,
        )

    def normalise(x):
        total = jnp.zeros((frames, 1), jnp.float32)
        for c in range(chunks):
            total = total + jnp.sum(x[c].astype(jnp.float32), axis=1, keepdims=True)
        center = total / width
        total = jnp.zeros((frames, 1), jnp.float32)
        for c in range(chunks):
            off = x[c].astype(jnp.float32) - center
            total = total + jnp.sum(off * off, axis=1, keepdims=True)
        scale = lax.rsqrt(total / width + 1e-05)
        for c in range(chunks):
            off = x[c].astype(jnp.float32) - center
            nrm[:, c * CW : (c + 1) * CW] = (off * scale).astype(jnp.bfloat16)

    def chunk(a, x, y, j):
        col = pl.multiple_of(j * CW, CW)
        gate_col = pl.multiple_of(half + j * CW, CW)
        value = jnp.dot(nrm[...], wv[a, :, pl.ds(col, CW)], preferred_element_type=jnp.float32)
        gate = jnp.dot(nrm[...], wv[a, :, pl.ds(gate_col, CW)], preferred_element_type=jnp.float32)
        glu = (value * jax.nn.sigmoid(gate)).astype(jnp.bfloat16).astype(jnp.float32)
        for h in range(CW // LANES):
            gbuf[h, PAD : PAD + frames, :] = glu[:, h * LANES : (h + 1) * LANES]
        for h in range(CW // LANES):
            lane = slice(h * LANES, (h + 1) * LANES)
            for r in range(0, frames, GROUP):
                mixed = jnp.zeros((GROUP, LANES), jnp.float32)
                for k in range(TAPS):
                    taps = kv[a, j * (CW // LANES) + h, k : k + 1, :]
                    mixed = mixed + gbuf[h, r + k + 1 : r + k + 1 + GROUP, :] * taps
                kept = x[r : r + GROUP, lane].astype(jnp.float32)
                y[r : r + GROUP, lane] = (kept + mixed * jax.nn.sigmoid(mixed)).astype(jnp.bfloat16)

    def one_utt(i, carry):
        m = i // CORES
        ours = lax.rem(i, CORES) == core

        @pl.when((s == 0) & jnp.logical_not(ours))
        def _():
            init_in(m).wait_recv()

        @pl.when(s > 0)
        def _():
            for j in range(mine):
                hop(i, j).wait_recv()
                forward(i, j).start()
            for j in range(mine):
                forward_in(i, j).wait_recv()

        normalise(xin.at[i])

        def chunk_a(j, carry):
            at = core * mine + j
            chunk(0, xin.at[i, at], xmid.at[i, at], j)
            middle(i, j).start()
            return carry

        lax.fori_loop(0, mine, chunk_a, 0)

        @pl.when(i == 0)
        def _():
            gather_3(1)
            taps_of(1)

        for j in range(mine):
            middle_in(i, j).wait_recv()
        normalise(xmid.at[i])

        def chunk_b(j, carry):
            at = core * mine + j
            chunk(1, xmid.at[i, at], obuf.at[i, j], j)

            @pl.when(s < last)
            def _():
                hop(i, j).start()

            @pl.when((s == last) & jnp.logical_not(ours))
            def _():
                final(i, j).start()

            return carry

        lax.fori_loop(0, mine, chunk_b, 0)

        @pl.when((s == last) & ours)
        def _():
            ctx = jnp.zeros((frames, wctx_ref.shape[1]), jnp.float32)
            for j in range(mine):
                at = pl.ds(pl.multiple_of((core * mine + j) * CW, CW), CW)
                ctx = ctx + jnp.dot(obuf[i, j], wctx_ref[at, :], preferred_element_type=jnp.float32)
            for j in range(mine):
                final(i, j).wait_recv()
                at = pl.ds(pl.multiple_of(((1 - core) * mine + j) * CW, CW), CW)
                ctx = ctx + jnp.dot(pbuf[m, j], wctx_ref[at, :], preferred_element_type=jnp.float32)
            size = jnp.sum(ctx * ctx, axis=1, keepdims=True)
            cbuf[m] = (ctx * lax.rsqrt(size + 1e-06)).astype(jnp.bfloat16)
            for j in range(sections - 1):
                scatter(m, j).start()

        return carry

    lax.fori_loop(0, utts, one_utt, 0)

    def score(m, carry):
        @pl.when(s < last)
        def _():
            scatter(m, 0).wait_recv()

        @pl.when(s == last)
        def _():
            enc[m] = cbuf[m, last * share : (last + 1) * share, :]

        spots = lax.broadcasted_iota(jnp.int32, (share, frames), 1)
        rows_at = lax.broadcasted_iota(jnp.int32, (share, frames), 0) + s * share
        sims = 10.0 * lax.dot_general(
            enc[m], tgt[m], (((1,), (1,)), ((), ())), preferred_element_type=jnp.float32
        )
        positive = jnp.sum(jnp.where(spots == rows_at, sims, 0.0), axis=1, keepdims=True)
        negative = jnp.sum(cnt[m] * jnp.exp(sims), axis=1, keepdims=True)
        out_ref[m] = jnp.log(jnp.exp(positive) + negative) - positive
        return carry

    lax.fori_loop(0, micro, score, 0)

    for t in range(2):
        for h in range(CORES):

            @pl.when(jnp.logical_not(stays[t] & (core == h)))
            def _():
                own_out(t, h).wait_send()

    for a in range(2):
        for n in range(7):
            ring_out(a, n).wait_send()

    @pl.when(s == 0)
    def _():
        for m in range(micro):
            init(m).wait_send()

    def drain(i, carry):
        for j in range(mine):
            middle(i, j).wait_send()

            @pl.when(s < last)
            def _():
                hop(i, j).wait_send()

            @pl.when(s > 0)
            def _():
                forward(i, j).wait_send()

            @pl.when((s == last) & (lax.rem(i, CORES) != core))
            def _():
                final(i, j).wait_send()

        return carry

    lax.fori_loop(0, utts, drain, 0)

    @pl.when(s == last)
    def _():
        for m in range(micro):
            for j in range(sections - 1):
                scatter(m, j).wait_send()


def relay(sections, columns, feats, wcat, w_ctx, w_tgt, embed, starts, picks):
    micro, frames, width = feats.shape
    chunks = width // CW
    share = frames // sections
    proj = w_ctx.shape[1]
    utts = CORES * micro
    mine = chunks // CORES
    half = width // CORES
    vmem = pl.BlockSpec(memory_space=pltpu.VMEM)
    smem = pl.BlockSpec(memory_space=pltpu.SMEM)
    dma = pltpu.SemaphoreType.DMA
    bf16 = jnp.bfloat16
    return pl.pallas_call(
        functools.partial(relay_kernel, sections, columns),
        out_shape=jax.ShapeDtypeStruct((micro, share, 1), jnp.float32),
        in_specs=[vmem, vmem, vmem, vmem, vmem, smem, vmem],
        out_specs=vmem,
        scratch_shapes=[
            pltpu.VMEM((utts, chunks, frames, CW), bf16),
            pltpu.VMEM((utts, chunks, frames, CW), bf16),
            pltpu.VMEM((utts, mine, frames, CW), bf16),
            pltpu.VMEM((micro, mine, frames, CW), bf16),
            pltpu.VMEM((frames, width), bf16),
            pltpu.VMEM((CW // LANES, frames + 2 * PAD, LANES), jnp.float32),
            pltpu.VMEM((2, width, wcat.shape[3]), bf16),
            pltpu.VMEM((2, half // LANES, 32, LANES), jnp.float32),
            pltpu.VMEM((micro, frames, proj), bf16),
            pltpu.VMEM((micro, share, frames), jnp.float32),
            pltpu.VMEM((micro, share, proj), bf16),
            pltpu.VMEM((micro, frames, proj), bf16),
            dma((2, CORES)),
            dma((2, CORES)),
            dma((2, 7)),
            dma((2, 7)),
            dma((micro,)),
            dma((micro,)),
            dma((utts, mine)),
            dma((utts, mine)),
            dma((utts, mine)),
            dma((utts, mine)),
            dma((utts, mine)),
            dma((utts, mine)),
            dma((micro, mine)),
            dma((micro, mine)),
            dma((micro, sections)),
            dma((micro,)),
        ],
        compiler_params=pltpu.CompilerParams(
            collective_id=0, has_side_effects=True, vmem_limit_bytes=60 << 20
        ),
    )(feats, wcat, w_ctx, w_tgt, embed, starts, picks)


def on_device(feats, w_in, dw_kernel, mask_embed, w_ctx, w_tgt, mask_starts, distractors):
    sections = lax.axis_size("section")
    columns = lax.axis_size("fsdp")
    width = feats.shape[3]
    half = width // CORES

    taps = dw_kernel[:, 0].transpose(0, 2, 1)
    taps = jnp.pad(taps, ((0, 0), (0, 0), (0, LANES - taps.shape[2])))
    rows = w_in[:, 0]
    wcat = jnp.stack(
        [
            jnp.concatenate(
                [
                    rows[:, :, h * half : (h + 1) * half],
                    rows[:, :, width + h * half : width + (h + 1) * half],
                    taps,
                ],
                axis=2,
            )
            for h in range(CORES)
        ],
        axis=1,
    )
    loss = relay(
        sections,
        columns,
        feats[:, 0],
        wcat,
        w_ctx,
        w_tgt,
        mask_embed[None, :],
        mask_starts[:, 0],
        distractors[:, 0],
    )
    return loss[:, :, 0][:, None, :]


def solution(mesh):
    placed = (
        P(None, "fsdp", None, None),
        P(None, "section", "fsdp", None),
        P(None, "section", None, "fsdp"),
        P(),
        P(),
        P(),
        P(None, "fsdp", None),
        P(None, "fsdp", "section", None),
    )
    return jax.shard_map(
        on_device, mesh=mesh, in_specs=placed, out_specs=P(None, "fsdp", "section"), check_vma=False
    )
```

time: 456 us -> 351 us (0.77); the launches traced: 451 us -> 351 us
  waiting for transfers between devices: 129 us -> 0 us
  Pallas kernels: 272 us -> 346 us
  between operations: 13.5 us -> 0.04 us
  other arithmetic: 13.5 us -> 2.79 us
  local copies, waits for them, and re-layouts: 10.8 us -> 2.05 us
  starting transfers between devices: 7.58 us -> 0 us
  matrix products: 4.71 us -> 0 us
    all_gather x1 -> x0, waiting for transfers between devices: 116 us -> none  [on_device(): weights = lax.all_gather(pair, 'fsdp', axis=1, tiled=True)]
    pallas_call x1, Pallas kernels: 272 us -> 346 us  [relay(): pl.pallas_call(functools.partial(relay_kernel, sections, columns), out_sh...]
    ppermute x2 -> x0, waiting for transfers between devices: 12.5 us -> none  [the longest x1 12.5 us: on_device(): got_2 = lax.ppermute(second, 'section', route_2)]
    ppermute x2 -> x0, starting transfers between devices: 7.58 us -> none  [the longest x1 5.86 us: on_device(): got_2 = lax.ppermute(second, 'section', route_2)]
    unnamed x12 -> x5, local copies, waits for them, and re-layouts: 5.72 us -> 0.14 us
    dot_general x1 -> x0, matrix products: 4.71 us -> none  [on_device(): jnp.einsum('mjd,de->mje', feats_local, w_tgt, preferred_element_type=jnp....]
    squeeze x1 -> x0, local copies, waits for them, and re-layouts: 4.7 us -> none  [on_device(): feats_local = feats[:, 0]]
  transfers between devices with their start and end apart: 3 -> 0, of which waited for: 2 -> 0; matrix products, arithmetic and copies ran while one was open for 5% -> 0% of each run, Pallas kernels for 0% -> 0%
where the time goes in v2:
time: 351 us
  Pallas kernels  346 us (99%)
    pallas_call x1, Pallas kernels, relay(): pl.pallas_call(functools.partial(relay_kernel, sections, columns), out_sh...  346 us

profile of v2, /device:TPU:1, one launch (start us, length us, event | category | flops | bytes accessed | tf_op | source)
XLA Modules:
  0.0 350.7 jit_solution(16674147603326669429)
XLA Ops:
  0.0 0.0 copy-start
  0.0 1.3 fusion.5
  1.3 0.0 copy-done
  1.3 0.1 copy.12
  1.5 0.1 fusion.4
  1.6 0.0 copy-start.1
  1.6 1.2 pad_maximum_fusion.wcat_ref
  2.8 0.0 copy-done.1
  2.8 0.6 broadcast_in_dim.3.embed_ref
  3.3 345.8 %shard_map.82 = f32[4,32,1]{2,1,0:T(8,128)} custom-call(bf16[4,256,1536]{2,1,0:T(8,128)(2,1)} %bitcast.16, bf16[2,2,96,1664]{3,2,1,0:T(8,128)(2,1)} %pad_maximum_fusion.wcat_ref, bf16[1536,768]{1,0:T(8,128)(2,1)} %wctx_ref.1, bf16[1536,768]{1,0:T(8,128)(2,1)} %wtgt_ref.1, bf16[1,1536]{1,0:T(2,128)(2,1)} %broadcast_in_dim.3.embed_ref, s32[4,12]{1,0:T(4,128)} %bitcast.20, ...), custom_call_target="tpu_custom_call" | custom-call | tf_op jit(solution)/shard_map/pallas_call | solution.py:490
  349.1 1.5 reduce
Async XLA Ops:
  0.0 1.3 copy-start
  1.6 1.2 copy-start.1

commit v3 on v2

--- a/solution.py
+++ b/solution.py
@@ -9,10 +9,9 @@
 
 MASK_LEN = 10
 TAPS = 31
-CW = 256
 LANES = 128
 PAD = 16
-GROUP = 64
+GROUP = 32
 CORES = 2
 MESH = pl.DeviceIdType.MESH
 
@@ -33,7 +32,8 @@
     obuf,
     pbuf,
     nrm,
-    gbuf,
+    gbuf_0,
+    gbuf_1,
     wv,
     kv,
     tgt,
@@ -60,7 +60,7 @@
     utts, chunks, frames, _ = xin.shape
     micro = utts // CORES
     mine = chunks // CORES
-    width = chunks * CW
+    width = chunks * LANES
     half = width // CORES
     share = frames // sections
     last = sections - 1
@@ -135,7 +135,8 @@
         )
 
     stays = [(s == 0), (s == last)]
-    for t in range(2):
+
+    def send_own(t):
         for h in range(CORES):
             here = stays[t] & (core == h)
 
@@ -146,6 +147,13 @@
             @pl.when(jnp.logical_not(here))
             def _():
                 own_out(t, h).start()
+
+    low = s < sections // 2
+    send_own(0)
+
+    @pl.when(jnp.logical_not(low))
+    def _():
+        send_own(1)
 
     def part(y_at, x_at):
         chip = lax.rem(y_at + 2 * ys, ys) * 2 + x_at
@@ -222,17 +230,17 @@
 
     @pl.when(s == 0)
     def _():
-        spot = lax.broadcasted_iota(jnp.int32, (frames, CW), 0)
+        spot = lax.broadcasted_iota(jnp.int32, (frames, LANES), 0)
 
         def one(m, carry):
-            covered = jnp.zeros((frames, CW), jnp.int32)
+            covered = jnp.zeros((frames, LANES), jnp.int32)
             for j in range(starts_ref.shape[1]):
                 start = starts_ref[m, j]
                 inside = (spot >= start) & (spot < start + MASK_LEN)
                 covered = jnp.where(inside, 1, covered)
             for c in range(chunks):
-                embed = embed_ref[:, c * CW : (c + 1) * CW].astype(jnp.float32)
-                seen = feats_ref[m, :, c * CW : (c + 1) * CW].astype(jnp.float32)
+                embed = embed_ref[:, c * LANES : (c + 1) * LANES].astype(jnp.float32)
+                seen = feats_ref[m, :, c * LANES : (c + 1) * LANES].astype(jnp.float32)
                 xin[CORES * m + core, c] = jnp.where(covered > 0, embed, seen).astype(jnp.bfloat16)
             init(m).start()
             return carry
@@ -250,13 +258,19 @@
         cnt[m] = total
         return carry
 
+    lax.fori_loop(0, micro, targets, 0)
     gather_2(0)
+
     gather_1(1)
-    lax.fori_loop(0, micro, targets, 0)
-
-    for b in range(CW // LANES):
-        gbuf[b, 0:PAD, :] = jnp.zeros((PAD, LANES), jnp.float32)
-        gbuf[b, PAD + frames : 2 * PAD + frames, :] = jnp.zeros((PAD, LANES), jnp.float32)
+
+    @pl.when(low)
+    def _():
+        send_own(1)
+
+
+    for g in (gbuf_0, gbuf_1):
+        g[0:PAD, :] = jnp.zeros((PAD, LANES), jnp.float32)
+        g[PAD + frames : 2 * PAD + frames, :] = jnp.zeros((PAD, LANES), jnp.float32)
 
     gather_2(1)
     gather_3(0)
@@ -321,25 +335,22 @@
         scale = lax.rsqrt(total / width + 1e-05)
         for c in range(chunks):
             off = x[c].astype(jnp.float32) - center
-            nrm[:, c * CW : (c + 1) * CW] = (off * scale).astype(jnp.bfloat16)
+            nrm[:, c * LANES : (c + 1) * LANES] = (off * scale).astype(jnp.bfloat16)
 
     def chunk(a, x, y, j):
-        col = pl.multiple_of(j * CW, CW)
-        gate_col = pl.multiple_of(half + j * CW, CW)
-        value = jnp.dot(nrm[...], wv[a, :, pl.ds(col, CW)], preferred_element_type=jnp.float32)
-        gate = jnp.dot(nrm[...], wv[a, :, pl.ds(gate_col, CW)], preferred_element_type=jnp.float32)
-        glu = (value * jax.nn.sigmoid(gate)).astype(jnp.bfloat16).astype(jnp.float32)
-        for h in range(CW // LANES):
-            gbuf[h, PAD : PAD + frames, :] = glu[:, h * LANES : (h + 1) * LANES]
-        for h in range(CW // LANES):
-            lane = slice(h * LANES, (h + 1) * LANES)
-            for r in range(0, frames, GROUP):
-                mixed = jnp.zeros((GROUP, LANES), jnp.float32)
-                for k in range(TAPS):
-                    taps = kv[a, j * (CW // LANES) + h, k : k + 1, :]
-                    mixed = mixed + gbuf[h, r + k + 1 : r + k + 1 + GROUP, :] * taps
-                kept = x[r : r + GROUP, lane].astype(jnp.float32)
-                y[r : r + GROUP, lane] = (kept + mixed * jax.nn.sigmoid(mixed)).astype(jnp.bfloat16)
+        g = (gbuf_0, gbuf_1)[j % 2]
+        col = 2 * LANES * j
+        proj = jnp.dot(
+            nrm[...], wv[a, :, col : col + 2 * LANES], preferred_element_type=jnp.float32
+        )
+        glu = (proj[:, :LANES] * jax.nn.sigmoid(proj[:, LANES:])).astype(jnp.bfloat16)
+        g[PAD : PAD + frames, :] = glu.astype(jnp.float32)
+        for r in range(0, frames, GROUP):
+            mixed = jnp.zeros((GROUP, LANES), jnp.float32)
+            for k in range(TAPS):
+                mixed = mixed + g[r + k + 1 : r + k + 1 + GROUP, :] * kv[a, j, k : k + 1, :]
+            kept = x[r : r + GROUP, :].astype(jnp.float32)
+            y[r : r + GROUP, :] = (kept + mixed * jax.nn.sigmoid(mixed)).astype(jnp.bfloat16)
 
     def one_utt(i, carry):
         m = i // CORES
@@ -359,13 +370,10 @@
 
         normalise(xin.at[i])
 
-        def chunk_a(j, carry):
+        for j in range(mine):
             at = core * mine + j
             chunk(0, xin.at[i, at], xmid.at[i, at], j)
             middle(i, j).start()
-            return carry
-
-        lax.fori_loop(0, mine, chunk_a, 0)
 
         @pl.when(i == 0)
         def _():
@@ -376,7 +384,7 @@
             middle_in(i, j).wait_recv()
         normalise(xmid.at[i])
 
-        def chunk_b(j, carry):
+        for j in range(mine):
             at = core * mine + j
             chunk(1, xmid.at[i, at], obuf.at[i, j], j)
 
@@ -388,19 +396,15 @@
             def _():
                 final(i, j).start()
 
-            return carry
-
-        lax.fori_loop(0, mine, chunk_b, 0)
-
         @pl.when((s == last) & ours)
         def _():
             ctx = jnp.zeros((frames, wctx_ref.shape[1]), jnp.float32)
             for j in range(mine):
-                at = pl.ds(pl.multiple_of((core * mine + j) * CW, CW), CW)
+                at = pl.ds(pl.multiple_of((core * mine + j) * LANES, LANES), LANES)
                 ctx = ctx + jnp.dot(obuf[i, j], wctx_ref[at, :], preferred_element_type=jnp.float32)
             for j in range(mine):
                 final(i, j).wait_recv()
-                at = pl.ds(pl.multiple_of(((1 - core) * mine + j) * CW, CW), CW)
+                at = pl.ds(pl.multiple_of(((1 - core) * mine + j) * LANES, LANES), LANES)
                 ctx = ctx + jnp.dot(pbuf[m, j], wctx_ref[at, :], preferred_element_type=jnp.float32)
             size = jnp.sum(ctx * ctx, axis=1, keepdims=True)
             cbuf[m] = (ctx * lax.rsqrt(size + 1e-06)).astype(jnp.bfloat16)
@@ -477,7 +481,7 @@
 
 def relay(sections, columns, feats, wcat, w_ctx, w_tgt, embed, starts, picks):
     micro, frames, width = feats.shape
-    chunks = width // CW
+    chunks = width // LANES
     share = frames // sections
     proj = w_ctx.shape[1]
     utts = CORES * micro
@@ -493,12 +497,13 @@
         in_specs=[vmem, vmem, vmem, vmem, vmem, smem, vmem],
         out_specs=vmem,
         scratch_shapes=[
-            pltpu.VMEM((utts, chunks, frames, CW), bf16),
-            pltpu.VMEM((utts, chunks, frames, CW), bf16),
-            pltpu.VMEM((utts, mine, frames, CW), bf16),
-            pltpu.VMEM((micro, mine, frames, CW), bf16),
+            pltpu.VMEM((utts, chunks, frames, LANES), bf16),
+            pltpu.VMEM((utts, chunks, frames, LANES), bf16),
+            pltpu.VMEM((utts, mine, frames, LANES), bf16),
+            pltpu.VMEM((micro, mine, frames, LANES), bf16),
             pltpu.VMEM((frames, width), bf16),
-            pltpu.VMEM((CW // LANES, frames + 2 * PAD, LANES), jnp.float32),
+            pltpu.VMEM((frames + 2 * PAD, LANES), jnp.float32),
+            pltpu.VMEM((frames + 2 * PAD, LANES), jnp.float32),
             pltpu.VMEM((2, width, wcat.shape[3]), bf16),
             pltpu.VMEM((2, half // LANES, 32, LANES), jnp.float32),
             pltpu.VMEM((micro, frames, proj), bf16),
@@ -536,21 +541,10 @@
 
     taps = dw_kernel[:, 0].transpose(0, 2, 1)
     taps = jnp.pad(taps, ((0, 0), (0, 0), (0, LANES - taps.shape[2])))
-    rows = w_in[:, 0]
-    wcat = jnp.stack(
-        [
-            jnp.concatenate(
-                [
-                    rows[:, :, h * half : (h + 1) * half],
-                    rows[:, :, width + h * half : width + (h + 1) * half],
-                    taps,
-                ],
-                axis=2,
-            )
-            for h in range(CORES)
-        ],
-        axis=1,
-    )
+    pairs = w_in[:, 0].reshape(2, -1, 2, CORES, half // LANES, LANES)
+    pairs = pairs.transpose(0, 3, 1, 4, 2, 5).reshape(2, CORES, -1, 2 * half)
+    taps = jnp.broadcast_to(taps[:, None], (2, CORES) + taps.shape[1:])
+    wcat = jnp.concatenate([pairs, taps], axis=3)
     loss = relay(
         sections,
         columns,

time: 351 us -> 375 us (1.068)
  Pallas kernels: 346 us -> 367 us
    pallas_call x1, Pallas kernels: 346 us -> 367 us  [relay(): pl.pallas_call(functools.partial(relay_kernel, sections, columns), out_sh...]
where the time goes in v3:
time: 375 us
  Pallas kernels  367 us (98%)
  local copies, waits for them, and re-layouts  5.52 us (1%)
    pallas_call x1, Pallas kernels, relay(): pl.pallas_call(functools.partial(relay_kernel, sections, columns), out_sh...  367 us

profile of v3, /device:TPU:1, one launch (start us, length us, event | category | flops | bytes accessed | tf_op | source)
XLA Modules:
  0.0 374.7 jit_solution(12531484478413531241)
XLA Ops:
  0.0 2.8 reshape_squeeze.3
  2.8 1.2 copy.12
  4.1 0.0 copy-start
  4.1 0.5 reshape.4
  4.6 0.2 copy-done
  4.8 0.1 copy.15
  5.0 0.0 copy-start.1
  5.0 1.1 pad_maximum_fusion.wcat_ref
  6.1 0.0 copy-done.1
  6.1 0.6 broadcast_in_dim.10.embed_ref
  6.7 366.5 %shard_map.82 = f32[4,32,1]{2,1,0:T(8,128)} custom-call(bf16[4,256,1536]{2,1,0:T(8,128)(2,1)} %bitcast.13, bf16[2,2,96,1664]{3,2,1,0:T(8,128)(2,1)} %pad_maximum_fusion.wcat_ref, bf16[1536,768]{1,0:T(8,128)(2,1)} %wctx_ref.1, bf16[1536,768]{1,0:T(8,128)(2,1)} %wtgt_ref.1, bf16[1,1536]{1,0:T(2,128)(2,1)} %broadcast_in_dim.10.embed_ref, s32[4,12]{1,0:T(4,128)} %bitcast.16, ...), custom_call_target="tpu_custom_call" | custom-call | tf_op jit(solution)/shard_map/pallas_call | solution.py:494
  373.2 1.5 reduce
  (2 shorter events, 0.0 us)
Async XLA Ops:
  4.1 0.7 copy-start
  5.0 1.2 copy-start.1

commit v4 on v2

--- a/solution.py
+++ b/solution.py
@@ -20,14 +20,18 @@
 def relay_kernel(
     sections,
     columns,
-    feats_ref,
+    feats_hbm,
     wcat_ref,
-    wctx_ref,
-    wtgt_ref,
+    wctx_hbm,
+    wtgt_hbm,
     embed_ref,
     starts_ref,
     picks_ref,
     out_ref,
+    feats_ref,
+    wctx_ref,
+    wtgt_ref,
+    load_sem,
     xin,
     xmid,
     obuf,
@@ -65,7 +69,6 @@
     share = frames // sections
     last = sections - 1
     rows = width // columns
-    piece = rows * CORES
     s = lax.axis_index("section")
     f = lax.axis_index("fsdp")
     core = lax.rem(f, 2)
@@ -78,6 +81,13 @@
     down = lax.rem(f + columns - 4, columns)
     nxt = lax.rem(s + 1, sections)
 
+    def load(src, dst, n):
+        return pltpu.make_async_copy(src, dst, load_sem.at[n])
+
+    load(feats_hbm, feats_ref, 0).start()
+    load(wtgt_hbm, wtgt_ref, 1).start()
+    load(wctx_hbm, wctx_ref, 2).start()
+
     barrier = pltpu.get_barrier_semaphore()
     for j in range(sections):
 
@@ -135,7 +145,8 @@
         )
 
     stays = [(s == 0), (s == last)]
-    for t in range(2):
+
+    def send_own(t):
         for h in range(CORES):
             here = stays[t] & (core == h)
 
@@ -147,68 +158,79 @@
             def _():
                 own_out(t, h).start()
 
-    def part(y_at, x_at):
+    low = s < sections // 2
+    send_own(0)
+
+    @pl.when(jnp.logical_not(low))
+    def _():
+        send_own(1)
+
+    def part(y_at, x_at, u):
         chip = lax.rem(y_at + 2 * ys, ys) * 2 + x_at
-        return pl.ds(pl.multiple_of(chip * piece, 64), piece)
-
-    def ring(a, n, y_at, x_at, column):
-        block = wv.at[a, part(y_at, x_at)]
-        return remote(block, block, ring_send.at[a, n], ring_recv.at[a, n], s, column)
+        return rows_of(CORES * chip + u)
+
+    def ring(a, n, u, y_at, x_at, column):
+        block = wv.at[a, part(y_at, x_at, u)]
+        return remote(block, block, ring_send.at[a, n, u], ring_recv.at[a, n, u], s, column)
 
     other = 1 - x_hi
 
-    def ring_out(a, n):
+    def ring_out(a, n, u):
         y_at, x_at, column = (
             (y, x_hi, across),
             (y, x_hi, up),
             (y, x_hi, down),
             (y, other, up),
             (y, other, down),
-            (y - 1, x_hi, up),
-            (y + 1, other, down),
+            (y - 1, x_hi, up) if u == 0 else (y + 1, x_hi, down),
+            (y + 2, x_hi, across),
         )[n]
-        return ring(a, n, y_at, x_at, column)
-
-    def ring_in(a, n):
+        return ring(a, n, u, y_at, x_at, column)
+
+    def ring_in(a, n, u):
         y_at, x_at, column = (
             (y, other, across),
             (y - 1, x_hi, up),
             (y + 1, x_hi, down),
             (y - 1, other, up),
             (y + 1, other, down),
-            (y - 2, x_hi, up),
-            (y + 2, other, down),
+            (y + 2, x_hi, up),
+            (y + 2, other, across),
         )[n]
-        return ring(a, n, y_at, x_at, column)
-
-    def gather_1(a):
-        for c in range(CORES):
-            t = a
-            here = stays[t] & (core == c)
+        return ring(a, n, u, y_at, x_at, column)
+
+    def ring_start(a):
+        for u in range(CORES):
+            here = stays[a] & (core == u)
 
             @pl.when(here)
             def _():
-                own_here(t, c).wait()
+                own_here(a, u).wait()
 
             @pl.when(jnp.logical_not(here))
             def _():
-                own_in(a, c).wait_recv()
-
-        for n in (0, 1, 2):
-            ring_out(a, n).start()
-
-    def gather_2(a):
-        ring_in(a, 0).wait_recv()
-        ring_out(a, 3).start()
-        ring_out(a, 4).start()
-        ring_in(a, 1).wait_recv()
-        ring_out(a, 5).start()
-        ring_in(a, 4).wait_recv()
-        ring_out(a, 6).start()
-
-    def gather_3(a):
-        for n in (2, 3, 5, 6):
-            ring_in(a, n).wait_recv()
+                own_in(a, u).wait_recv()
+
+            for n in (0, 1, 2):
+                ring_out(a, n, u).start()
+
+    def pass_on(a, u, arrived, then):
+        ring_in(a, arrived, u).wait_recv()
+        for n in then:
+            ring_out(a, n, u).start()
+
+    def ring_pass(a):
+        pass_on(a, 0, 1, (5,))
+        pass_on(a, 1, 2, (5,))
+        pass_on(a, 0, 0, (3, 4))
+        pass_on(a, 1, 0, (3, 4))
+        pass_on(a, 0, 5, (6,))
+        pass_on(a, 1, 5, (6,))
+
+    def ring_end(a):
+        for u in range(CORES):
+            for n in (2 - u, 3, 4, 6):
+                ring_in(a, n, u).wait_recv()
 
     def init(m):
         at = xin.at[CORES * m + core]
@@ -218,7 +240,28 @@
         at = xin.at[CORES * m + 1 - core]
         return remote(at, at, init_send.at[m], init_recv.at[m], s, peer)
 
-    gather_1(0)
+    ring_start(0)
+
+    def targets(m, carry):
+        proj = jnp.dot(feats_ref[m], wtgt_ref[...], preferred_element_type=jnp.float32)
+        size = jnp.sum(proj * proj, axis=1, keepdims=True)
+        tgt[m] = (proj * lax.rsqrt(size + 1e-06)).astype(jnp.bfloat16)
+        spots = lax.broadcasted_iota(jnp.int32, (share, frames), 1)
+        total = jnp.zeros((share, frames), jnp.float32)
+        for k in range(picks_ref.shape[2]):
+            total = total + jnp.where(picks_ref[m, :, k : k + 1] == spots, 1.0, 0.0)
+        cnt[m] = total
+        return carry
+
+    load(feats_hbm, feats_ref, 0).wait()
+    load(wtgt_hbm, wtgt_ref, 1).wait()
+    lax.fori_loop(0, micro, targets, 0)
+    ring_pass(0)
+    ring_start(1)
+
+    @pl.when(low)
+    def _():
+        send_own(1)
 
     @pl.when(s == 0)
     def _():
@@ -239,27 +282,14 @@
 
         lax.fori_loop(0, micro, one, 0)
 
-    def targets(m, carry):
-        proj = jnp.dot(feats_ref[m], wtgt_ref[...], preferred_element_type=jnp.float32)
-        size = jnp.sum(proj * proj, axis=1, keepdims=True)
-        tgt[m] = (proj * lax.rsqrt(size + 1e-06)).astype(jnp.bfloat16)
-        spots = lax.broadcasted_iota(jnp.int32, (share, frames), 1)
-        total = jnp.zeros((share, frames), jnp.float32)
-        for k in range(picks_ref.shape[2]):
-            total = total + jnp.where(picks_ref[m, :, k : k + 1] == spots, 1.0, 0.0)
-        cnt[m] = total
-        return carry
-
-    gather_2(0)
-    gather_1(1)
-    lax.fori_loop(0, micro, targets, 0)
 
     for b in range(CW // LANES):
         gbuf[b, 0:PAD, :] = jnp.zeros((PAD, LANES), jnp.float32)
         gbuf[b, PAD + frames : 2 * PAD + frames, :] = jnp.zeros((PAD, LANES), jnp.float32)
 
-    gather_2(1)
-    gather_3(0)
+    ring_pass(1)
+    load(wctx_hbm, wctx_ref, 2).wait()
+    ring_end(0)
 
     def taps_of(a):
         for h in range(half // LANES):
@@ -369,7 +399,7 @@
 
         @pl.when(i == 0)
         def _():
-            gather_3(1)
+            ring_end(1)
             taps_of(1)
 
         for j in range(mine):
@@ -441,7 +471,8 @@
 
     for a in range(2):
         for n in range(7):
-            ring_out(a, n).wait_send()
+            for u in range(CORES):
+                ring_out(a, n, u).wait_send()
 
     @pl.when(s == 0)
     def _():
@@ -485,14 +516,19 @@
     half = width // CORES
     vmem = pl.BlockSpec(memory_space=pltpu.VMEM)
     smem = pl.BlockSpec(memory_space=pltpu.SMEM)
+    hbm = pl.BlockSpec(memory_space=pl.ANY)
     dma = pltpu.SemaphoreType.DMA
     bf16 = jnp.bfloat16
     return pl.pallas_call(
         functools.partial(relay_kernel, sections, columns),
         out_shape=jax.ShapeDtypeStruct((micro, share, 1), jnp.float32),
-        in_specs=[vmem, vmem, vmem, vmem, vmem, smem, vmem],
+        in_specs=[hbm, hbm, hbm, hbm, vmem, smem, vmem],
         out_specs=vmem,
         scratch_shapes=[
+            pltpu.VMEM(feats.shape, bf16),
+            pltpu.VMEM(w_ctx.shape, bf16),
+            pltpu.VMEM(w_tgt.shape, bf16),
+            dma((3,)),
             pltpu.VMEM((utts, chunks, frames, CW), bf16),
             pltpu.VMEM((utts, chunks, frames, CW), bf16),
             pltpu.VMEM((utts, mine, frames, CW), bf16),
@@ -507,8 +543,8 @@
             pltpu.VMEM((micro, frames, proj), bf16),
             dma((2, CORES)),
             dma((2, CORES)),
-            dma((2, 7)),
-            dma((2, 7)),
+            dma((2, 7, CORES)),
+            dma((2, 7, CORES)),
             dma((micro,)),
             dma((micro,)),
             dma((utts, mine)),

time: 351 us -> 331 us (0.943)
  Pallas kernels: 346 us -> 326 us
    pallas_call x1, Pallas kernels: 346 us -> 326 us  [relay(): pl.pallas_call(functools.partial(relay_kernel, sections, columns), out_sh...]
where the time goes in v4:
time: 331 us; the launch traced here: 330 us
  Pallas kernels  326 us (98%)
    pallas_call x1, Pallas kernels, relay(): pl.pallas_call(functools.partial(relay_kernel, sections, columns), out_sh...  326 us

profile of v4, /device:TPU:1, one launch (start us, length us, event | category | flops | bytes accessed | tf_op | source)
XLA Modules:
  0.0 330.5 jit_solution(12806632435533105618)
XLA Ops:
  0.0 0.0 copy-start
  0.0 1.3 fusion.5
  1.3 0.0 copy-done
  1.3 0.1 copy.12
  1.5 0.1 fusion.4
  1.6 0.0 copy-start.1
  1.6 1.2 pad_maximum_fusion.wcat_ref
  2.8 0.0 copy-done.1
  2.8 0.6 broadcast_in_dim.3.embed_ref
  3.3 325.6 %shard_map.82 = f32[4,32,1]{2,1,0:T(8,128)} custom-call(bf16[4,256,1536]{2,1,0:T(8,128)(2,1)} %bitcast.16, bf16[2,2,96,1664]{3,2,1,0:T(8,128)(2,1)} %pad_maximum_fusion.wcat_ref, bf16[1536,768]{1,0:T(8,128)(2,1)} %wctx_hbm.1, bf16[1536,768]{1,0:T(8,128)(2,1)} %wtgt_hbm.1, bf16[1,1536]{1,0:T(2,128)(2,1)} %broadcast_in_dim.3.embed_ref, s32[4,12]{1,0:T(4,128)} %bitcast.20, ...), custom_call_target="tpu_custom_call" | custom-call | tf_op jit(solution)/shard_map/pallas_call | solution.py:522
  328.9 1.5 reduce
Async XLA Ops:
  0.0 1.3 copy-start
  1.6 1.2 copy-start.1

commit v5 on v4

--- a/solution.py
+++ b/solution.py
@@ -32,12 +32,10 @@
     wctx_ref,
     wtgt_ref,
     load_sem,
-    xin,
-    xmid,
-    obuf,
-    pbuf,
-    nrm,
+    xall,
+    part_sum,
     gbuf,
+    wsum,
     wv,
     kv,
     tgt,
@@ -52,20 +50,15 @@
     init_recv,
     hop_send,
     hop_recv,
-    fwd_send,
-    fwd_recv,
-    mid_send,
-    mid_recv,
-    fin_send,
-    fin_recv,
+    swap_send,
+    swap_recv,
     csend_sem,
     crecv_sem,
 ):
-    utts, chunks, frames, _ = xin.shape
+    _, utts, _, frames, half = xall.shape
     micro = utts // CORES
-    mine = chunks // CORES
-    width = chunks * CW
-    half = width // CORES
+    mine = half // CW
+    width = half * CORES
     share = frames // sections
     last = sections - 1
     rows = width // columns
@@ -158,12 +151,8 @@
             def _():
                 own_out(t, h).start()
 
-    low = s < sections // 2
     send_own(0)
-
-    @pl.when(jnp.logical_not(low))
-    def _():
-        send_own(1)
+    send_own(1)
 
     def part(y_at, x_at, u):
         chip = lax.rem(y_at + 2 * ys, ys) * 2 + x_at
@@ -233,11 +222,11 @@
                 ring_in(a, n, u).wait_recv()
 
     def init(m):
-        at = xin.at[CORES * m + core]
+        at = xall.at[0, CORES * m + core]
         return remote(at, at, init_send.at[m], init_recv.at[m], s, peer)
 
     def init_in(m):
-        at = xin.at[CORES * m + 1 - core]
+        at = xall.at[0, CORES * m + 1 - core]
         return remote(at, at, init_send.at[m], init_recv.at[m], s, peer)
 
     ring_start(0)
@@ -259,10 +248,6 @@
     ring_pass(0)
     ring_start(1)
 
-    @pl.when(low)
-    def _():
-        send_own(1)
-
     @pl.when(s == 0)
     def _():
         spot = lax.broadcasted_iota(jnp.int32, (frames, CW), 0)
@@ -273,10 +258,13 @@
                 start = starts_ref[m, j]
                 inside = (spot >= start) & (spot < start + MASK_LEN)
                 covered = jnp.where(inside, 1, covered)
-            for c in range(chunks):
+            for c in range(width // CW):
                 embed = embed_ref[:, c * CW : (c + 1) * CW].astype(jnp.float32)
                 seen = feats_ref[m, :, c * CW : (c + 1) * CW].astype(jnp.float32)
-                xin[CORES * m + core, c] = jnp.where(covered > 0, embed, seen).astype(jnp.bfloat16)
+                at = slice(c % mine * CW, (c % mine + 1) * CW)
+                xall[0, CORES * m + core, c // mine, :, at] = jnp.where(
+                    covered > 0, embed, seen
+                ).astype(jnp.bfloat16)
             init(m).start()
             return carry
 
@@ -291,43 +279,38 @@
     load(wctx_hbm, wctx_ref, 2).wait()
     ring_end(0)
 
-    def taps_of(a):
+    def prepare(a):
         for h in range(half // LANES):
             at = pl.ds(pl.multiple_of(core * half + h * LANES, LANES), LANES)
             block = wv[a, at, 2 * half : 2 * half + LANES]
             kv[a, h] = block.astype(jnp.float32).T[0:32, :]
-
-    taps_of(0)
+        ones = jnp.ones((8, width), jnp.bfloat16)
+        for c in range(2 * mine):
+            at = slice(c * CW, (c + 1) * CW)
+            wsum[a, :, at] = jnp.dot(ones, wv[a, :, at], preferred_element_type=jnp.float32)
+
+    prepare(0)
+
+    def piece(a, i, c, j):
+        return xall.at[a, i, c, :, pl.ds(j * CW, CW)]
 
     def hop(i, j):
         return remote(
-            obuf.at[i, j],
-            xin.at[i, core * mine + j],
+            piece(2, i, core, j),
+            piece(0, i, core, j),
             hop_send.at[i, j],
             hop_recv.at[i, j],
             nxt,
             f,
         )
 
-    def forward(i, j):
-        at = xin.at[i, core * mine + j]
-        return remote(at, at, fwd_send.at[i, j], fwd_recv.at[i, j], s, peer)
-
-    def forward_in(i, j):
-        at = xin.at[i, (1 - core) * mine + j]
-        return remote(at, at, fwd_send.at[i, j], fwd_recv.at[i, j], s, peer)
-
-    def middle(i, j):
-        at = xmid.at[i, core * mine + j]
-        return remote(at, at, mid_send.at[i, j], mid_recv.at[i, j], s, peer)
-
-    def middle_in(i, j):
-        at = xmid.at[i, (1 - core) * mine + j]
-        return remote(at, at, mid_send.at[i, j], mid_recv.at[i, j], s, peer)
-
-    def final(i, j):
-        m = i // CORES
-        return remote(obuf.at[i, j], pbuf.at[m, j], fin_send.at[m, j], fin_recv.at[m, j], s, peer)
+    def swap(a, i, j, c):
+        at = piece(a, i, c, j)
+        return remote(at, at, swap_send.at[a, i, j], swap_recv.at[a, i, j], s, peer)
+
+    def swap_in(a, i):
+        for j in range(mine):
+            swap(a, i, j, 1 - core).wait_recv()
 
     def scatter(m, j):
         return remote(
@@ -339,101 +322,124 @@
             f,
         )
 
-    def normalise(x):
-        total = jnp.zeros((frames, 1), jnp.float32)
-        for c in range(chunks):
-            total = total + jnp.sum(x[c].astype(jnp.float32), axis=1, keepdims=True)
-        center = total / width
-        total = jnp.zeros((frames, 1), jnp.float32)
-        for c in range(chunks):
-            off = x[c].astype(jnp.float32) - center
-            total = total + jnp.sum(off * off, axis=1, keepdims=True)
-        scale = lax.rsqrt(total / width + 1e-05)
-        for c in range(chunks):
-            off = x[c].astype(jnp.float32) - center
-            nrm[:, c * CW : (c + 1) * CW] = (off * scale).astype(jnp.bfloat16)
-
-    def chunk(a, x, y, j):
-        col = pl.multiple_of(j * CW, CW)
-        gate_col = pl.multiple_of(half + j * CW, CW)
-        value = jnp.dot(nrm[...], wv[a, :, pl.ds(col, CW)], preferred_element_type=jnp.float32)
-        gate = jnp.dot(nrm[...], wv[a, :, pl.ds(gate_col, CW)], preferred_element_type=jnp.float32)
-        glu = (value * jax.nn.sigmoid(gate)).astype(jnp.bfloat16).astype(jnp.float32)
-        for h in range(CW // LANES):
-            gbuf[h, PAD : PAD + frames, :] = glu[:, h * LANES : (h + 1) * LANES]
-        for h in range(CW // LANES):
-            lane = slice(h * LANES, (h + 1) * LANES)
-            for r in range(0, frames, GROUP):
-                mixed = jnp.zeros((GROUP, LANES), jnp.float32)
-                for k in range(TAPS):
-                    taps = kv[a, j * (CW // LANES) + h, k : k + 1, :]
-                    mixed = mixed + gbuf[h, r + k + 1 : r + k + 1 + GROUP, :] * taps
-                kept = x[r : r + GROUP, lane].astype(jnp.float32)
-                y[r : r + GROUP, lane] = (kept + mixed * jax.nn.sigmoid(mixed)).astype(jnp.bfloat16)
+    def row_sum(v):
+        return jnp.sum(v, axis=1, keepdims=True)
 
     def one_utt(i, carry):
         m = i // CORES
         ours = lax.rem(i, CORES) == core
 
-        @pl.when((s == 0) & jnp.logical_not(ours))
-        def _():
-            init_in(m).wait_recv()
-
-        @pl.when(s > 0)
-        def _():
+        def layer(a, carry):
+            @pl.when((s == 0) & (a == 0) & jnp.logical_not(ours))
+            def _():
+                init_in(m).wait_recv()
+
+            @pl.when((s > 0) & (a == 0))
+            def _():
+                for j in range(mine):
+                    hop(i, j).wait_recv()
+                    swap(0, i, j, core).start()
+
+            @pl.when((i == 0) & (a == 1))
+            def _():
+                ring_end(1)
+                prepare(1)
+
+            def product(c, col):
+                at = pl.ds(pl.multiple_of(c * half, CW), half)
+                return jnp.dot(
+                    xall[a, i, c], wv[a, at, col], preferred_element_type=jnp.float32
+                )
+
+            def columns_of(j):
+                value = pl.ds(j * CW, CW)
+                gate = pl.ds(half + j * CW, CW)
+                return value, gate
+
+            def first(j, carry):
+                value, gate = columns_of(j)
+                part_sum[j, 0] = product(core, value)
+                part_sum[j, 1] = product(core, gate)
+                return carry
+
             for j in range(mine):
-                hop(i, j).wait_recv()
-                forward(i, j).start()
+                first(j, 0)
+            def block(c, j):
+                return xall[a, i, c, :, j * CW : (j + 1) * CW].astype(jnp.float32)
+
+            total = jnp.zeros((frames, 1), jnp.float32)
             for j in range(mine):
-                forward_in(i, j).wait_recv()
-
-        normalise(xin.at[i])
-
-        def chunk_a(j, carry):
-            at = core * mine + j
-            chunk(0, xin.at[i, at], xmid.at[i, at], j)
-            middle(i, j).start()
+                total = total + row_sum(block(core, j))
+            base = total / half
+            square = jnp.zeros((frames, 1), jnp.float32)
+            for j in range(mine):
+                off = block(core, j) - base
+                square = square + row_sum(off * off)
+
+            @pl.when((s > 0) | (a > 0))
+            def _():
+                swap_in(a, i)
+
+            moved = jnp.zeros((frames, CW), jnp.float32)
+            far = jnp.zeros((frames, CW), jnp.float32)
+            for j in range(mine):
+                off = block(1 - core, j) - base
+                moved = moved + off
+                far = far + off * off
+            shift = row_sum(moved) / width
+            center = base + shift
+            spread = (square + row_sum(far)) / width - shift * shift
+            scale = lax.rsqrt(spread + 1e-05)
+
+            def second(j, carry):
+                value, gate = columns_of(j)
+                v = part_sum[j, 0] + product(1 - core, value)
+                v = (v - center * wsum[a, 0:1, value]) * scale
+                g = part_sum[j, 1] + product(1 - core, gate)
+                g = (g - center * wsum[a, 0:1, gate]) * scale
+                glu = (v * jax.nn.sigmoid(g)).astype(jnp.bfloat16).astype(jnp.float32)
+                for h in range(CW // LANES):
+                    gbuf[h, PAD : PAD + frames, :] = glu[:, h * LANES : (h + 1) * LANES]
+                for h in range(CW // LANES):
+                    lane = pl.ds(j * CW + h * LANES, LANES)
+                    for r in range(0, frames, GROUP):
+                        mixed = jnp.zeros((GROUP, LANES), jnp.float32)
+                        for k in range(TAPS):
+                            taps = kv[a, j * (CW // LANES) + h, k : k + 1, :]
+                            mixed = mixed + gbuf[h, r + k + 1 : r + k + 1 + GROUP, :] * taps
+                        kept = xall[a, i, core, r : r + GROUP, lane].astype(jnp.float32)
+                        xall[a + 1, i, core, r : r + GROUP, lane] = (
+                            kept + mixed * jax.nn.sigmoid(mixed)
+                        ).astype(jnp.bfloat16)
+
+                @pl.when((a == 0) | ((s == last) & jnp.logical_not(ours)))
+                def _():
+                    swap(a + 1, i, j, core).start()
+
+                @pl.when((a == 1) & (s < last))
+                def _():
+                    hop(i, j).start()
+
+                return carry
+
+            for j in range(mine):
+                second(j, 0)
             return carry
 
-        lax.fori_loop(0, mine, chunk_a, 0)
-
-        @pl.when(i == 0)
-        def _():
-            ring_end(1)
-            taps_of(1)
-
-        for j in range(mine):
-            middle_in(i, j).wait_recv()
-        normalise(xmid.at[i])
-
-        def chunk_b(j, carry):
-            at = core * mine + j
-            chunk(1, xmid.at[i, at], obuf.at[i, j], j)
-
-            @pl.when(s < last)
-            def _():
-                hop(i, j).start()
-
-            @pl.when((s == last) & jnp.logical_not(ours))
-            def _():
-                final(i, j).start()
-
-            return carry
-
-        lax.fori_loop(0, mine, chunk_b, 0)
+        lax.fori_loop(0, 2, layer, 0)
 
         @pl.when((s == last) & ours)
         def _():
-            ctx = jnp.zeros((frames, wctx_ref.shape[1]), jnp.float32)
-            for j in range(mine):
-                at = pl.ds(pl.multiple_of((core * mine + j) * CW, CW), CW)
-                ctx = ctx + jnp.dot(obuf[i, j], wctx_ref[at, :], preferred_element_type=jnp.float32)
-            for j in range(mine):
-                final(i, j).wait_recv()
-                at = pl.ds(pl.multiple_of(((1 - core) * mine + j) * CW, CW), CW)
-                ctx = ctx + jnp.dot(pbuf[m, j], wctx_ref[at, :], preferred_element_type=jnp.float32)
-            size = jnp.sum(ctx * ctx, axis=1, keepdims=True)
-            cbuf[m] = (ctx * lax.rsqrt(size + 1e-06)).astype(jnp.bfloat16)
+            def project(c):
+                at = pl.ds(pl.multiple_of(c * half, CW), half)
+                return jnp.dot(
+                    xall[2, i, c], wctx_ref[at, :], preferred_element_type=jnp.float32
+                )
+
+            ctx = project(core)
+            swap_in(2, i)
+            ctx = ctx + project(1 - core)
+            cbuf[m] = (ctx * lax.rsqrt(row_sum(ctx * ctx) + 1e-06)).astype(jnp.bfloat16)
             for j in range(sections - 1):
                 scatter(m, j).start()
 
@@ -481,7 +487,7 @@
 
     def drain(i, carry):
         for j in range(mine):
-            middle(i, j).wait_send()
+            swap(1, i, j, core).wait_send()
 
             @pl.when(s < last)
             def _():
@@ -489,11 +495,11 @@
 
             @pl.when(s > 0)
             def _():
-                forward(i, j).wait_send()
+                swap(0, i, j, core).wait_send()
 
             @pl.when((s == last) & (lax.rem(i, CORES) != core))
             def _():
-                final(i, j).wait_send()
+                swap(2, i, j, core).wait_send()
 
         return carry
 
@@ -508,12 +514,11 @@
 
 def relay(sections, columns, feats, wcat, w_ctx, w_tgt, embed, starts, picks):
     micro, frames, width = feats.shape
-    chunks = width // CW
     share = frames // sections
     proj = w_ctx.shape[1]
     utts = CORES * micro
-    mine = chunks // CORES
     half = width // CORES
+    mine = half // CW
     vmem = pl.BlockSpec(memory_space=pltpu.VMEM)
     smem = pl.BlockSpec(memory_space=pltpu.SMEM)
     hbm = pl.BlockSpec(memory_space=pl.ANY)
@@ -529,12 +534,10 @@
             pltpu.VMEM(w_ctx.shape, bf16),
             pltpu.VMEM(w_tgt.shape, bf16),
             dma((3,)),
-            pltpu.VMEM((utts, chunks, frames, CW), bf16),
-            pltpu.VMEM((utts, chunks, frames, CW), bf16),
-            pltpu.VMEM((utts, mine, frames, CW), bf16),
-            pltpu.VMEM((micro, mine, frames, CW), bf16),
-            pltpu.VMEM((frames, width), bf16),
+            pltpu.VMEM((3, utts, CORES, frames, half), bf16),
+            pltpu.VMEM((mine, 2, frames, CW), jnp.float32),
             pltpu.VMEM((CW // LANES, frames + 2 * PAD, LANES), jnp.float32),
+            pltpu.VMEM((2, 8, 2 * half), jnp.float32),
             pltpu.VMEM((2, width, wcat.shape[3]), bf16),
             pltpu.VMEM((2, half // LANES, 32, LANES), jnp.float32),
             pltpu.VMEM((micro, frames, proj), bf16),
@@ -549,12 +552,8 @@
             dma((micro,)),
             dma((utts, mine)),
             dma((utts, mine)),
-            dma((utts, mine)),
-            dma((utts, mine)),
-            dma((utts, mine)),
-            dma((utts, mine)),
-            dma((micro, mine)),
-            dma((micro, mine)),
+            dma((3, utts, mine)),
+            dma((3, utts, mine)),
             dma((micro, sections)),
             dma((micro,)),
         ],

time: 331 us -> 306 us (0.924)
  Pallas kernels: 326 us -> 301 us
    pallas_call x1, Pallas kernels: 326 us -> 301 us  [relay(): pl.pallas_call(functools.partial(relay_kernel, sections, columns), out_sh...]
where the time goes in v5:
time: 306 us
  Pallas kernels  301 us (98%)
    pallas_call x1, Pallas kernels, relay(): pl.pallas_call(functools.partial(relay_kernel, sections, columns), out_sh...  301 us

profile of v5, /device:TPU:1, one launch (start us, length us, event | category | flops | bytes accessed | tf_op | source)
XLA Modules:
  0.0 305.9 jit_solution(7788887797288531015)
XLA Ops:
  0.0 0.0 copy-start
  0.0 1.3 fusion.5
  1.3 0.0 copy-done
  1.3 0.1 copy.12
  1.5 0.1 fusion.4
  1.6 0.0 copy-start.1
  1.6 1.2 pad_maximum_fusion.wcat_ref
  2.8 0.0 copy-done.1
  2.8 0.6 broadcast_in_dim.3.embed_ref
  3.3 301.1 %shard_map.82 = f32[4,32,1]{2,1,0:T(8,128)} custom-call(bf16[4,256,1536]{2,1,0:T(8,128)(2,1)} %bitcast.16, bf16[2,2,96,1664]{3,2,1,0:T(8,128)(2,1)} %pad_maximum_fusion.wcat_ref, bf16[1536,768]{1,0:T(8,128)(2,1)} %wctx_hbm.1, bf16[1536,768]{1,0:T(8,128)(2,1)} %wtgt_hbm.1, bf16[1,1536]{1,0:T(2,128)(2,1)} %broadcast_in_dim.3.embed_ref, s32[4,12]{1,0:T(4,128)} %bitcast.20, ...), custom_call_target="tpu_custom_call" | custom-call | tf_op jit(solution)/shard_map/pallas_call | solution.py:527
  304.4 1.5 reduce
Async XLA Ops:
  0.0 1.3 copy-start
  1.6 1.2 copy-start.1

commit v6 on v5

--- a/solution.py
+++ b/solution.py
@@ -41,7 +41,6 @@
     tgt,
     cnt,
     enc,
-    cbuf,
     own_send,
     own_recv,
     ring_send,
@@ -312,14 +311,24 @@
         for j in range(mine):
             swap(a, i, j, 1 - core).wait_recv()
 
-    def scatter(m, j):
+    def scatter(i, j):
         return remote(
-            cbuf.at[m, pl.ds(j * share, share)],
-            enc.at[m],
-            csend_sem.at[m, j],
-            crecv_sem.at[m],
+            xall.at[2, i, core, pl.ds(j * share, share)],
+            enc.at[i // CORES, core],
+            csend_sem.at[i, j],
+            crecv_sem.at[i // CORES, core],
             j,
-            f,
+            f - core + lax.rem(i, CORES),
+        )
+
+    def scatter_in(m, c):
+        return remote(
+            xall.at[2, 0, 0, pl.ds(0, share)],
+            enc.at[m, c],
+            csend_sem.at[0, 0],
+            crecv_sem.at[m, c],
+            s,
+            peer,
         )
 
     def row_sum(v):
@@ -412,9 +421,9 @@
                             kept + mixed * jax.nn.sigmoid(mixed)
                         ).astype(jnp.bfloat16)
 
-                @pl.when((a == 0) | ((s == last) & jnp.logical_not(ours)))
+                @pl.when(a == 0)
                 def _():
-                    swap(a + 1, i, j, core).start()
+                    swap(1, i, j, core).start()
 
                 @pl.when((a == 1) & (s < last))
                 def _():
@@ -428,20 +437,14 @@
 
         lax.fori_loop(0, 2, layer, 0)
 
-        @pl.when((s == last) & ours)
+        @pl.when(s == last)
         def _():
-            def project(c):
-                at = pl.ds(pl.multiple_of(c * half, CW), half)
-                return jnp.dot(
-                    xall[2, i, c], wctx_ref[at, :], preferred_element_type=jnp.float32
-                )
-
-            ctx = project(core)
-            swap_in(2, i)
-            ctx = ctx + project(1 - core)
-            cbuf[m] = (ctx * lax.rsqrt(row_sum(ctx * ctx) + 1e-06)).astype(jnp.bfloat16)
-            for j in range(sections - 1):
-                scatter(m, j).start()
+            for j in range(last):
+                scatter(i, j).start()
+
+            @pl.when(jnp.logical_not(ours))
+            def _():
+                scatter(i, last).start()
 
         return carry
 
@@ -450,16 +453,25 @@
     def score(m, carry):
         @pl.when(s < last)
         def _():
-            scatter(m, 0).wait_recv()
+            scatter_in(m, core).wait_recv()
 
         @pl.when(s == last)
         def _():
-            enc[m] = cbuf[m, last * share : (last + 1) * share, :]
-
+            enc[m, core] = xall[2, CORES * m + core, core, last * share : (last + 1) * share, :]
+
+        scatter_in(m, 1 - core).wait_recv()
+        ctx = jnp.zeros((share, wctx_ref.shape[1]), jnp.float32)
+        for c in range(CORES):
+            ctx = ctx + jnp.dot(
+                enc[m, c],
+                wctx_ref[c * half : (c + 1) * half, :],
+                preferred_element_type=jnp.float32,
+            )
+        ctx = (ctx * lax.rsqrt(row_sum(ctx * ctx) + 1e-06)).astype(jnp.bfloat16)
         spots = lax.broadcasted_iota(jnp.int32, (share, frames), 1)
         rows_at = lax.broadcasted_iota(jnp.int32, (share, frames), 0) + s * share
         sims = 10.0 * lax.dot_general(
-            enc[m], tgt[m], (((1,), (1,)), ((), ())), preferred_element_type=jnp.float32
+            ctx, tgt[m], (((1,), (1,)), ((), ())), preferred_element_type=jnp.float32
         )
         positive = jnp.sum(jnp.where(spots == rows_at, sims, 0.0), axis=1, keepdims=True)
         negative = jnp.sum(cnt[m] * jnp.exp(sims), axis=1, keepdims=True)
@@ -497,19 +509,18 @@
             def _():
                 swap(0, i, j, core).wait_send()
 
-            @pl.when((s == last) & (lax.rem(i, CORES) != core))
-            def _():
-                swap(2, i, j, core).wait_send()
+        @pl.when(s == last)
+        def _():
+            for j in range(last):
+                scatter(i, j).wait_send()
+
+            @pl.when(lax.rem(i, CORES) != core)
+            def _():
+                scatter(i, last).wait_send()
 
         return carry
 
     lax.fori_loop(0, utts, drain, 0)
-
-    @pl.when(s == last)
-    def _():
-        for m in range(micro):
-            for j in range(sections - 1):
-                scatter(m, j).wait_send()
 
 
 def relay(sections, columns, feats, wcat, w_ctx, w_tgt, embed, starts, picks):
@@ -542,8 +553,7 @@
             pltpu.VMEM((2, half // LANES, 32, LANES), jnp.float32),
             pltpu.VMEM((micro, frames, proj), bf16),
             pltpu.VMEM((micro, share, frames), jnp.float32),
-            pltpu.VMEM((micro, share, proj), bf16),
-            pltpu.VMEM((micro, frames, proj), bf16),
+            pltpu.VMEM((micro, CORES, share, half), bf16),
             dma((2, CORES)),
             dma((2, CORES)),
             dma((2, 7, CORES)),
@@ -552,10 +562,10 @@
             dma((micro,)),
             dma((utts, mine)),
             dma((utts, mine)),
-            dma((3, utts, mine)),
-            dma((3, utts, mine)),
-            dma((micro, sections)),
-            dma((micro,)),
+            dma((2, utts, mine)),
+            dma((2, utts, mine)),
+            dma((utts, sections)),
+            dma((micro, CORES)),
         ],
         compiler_params=pltpu.CompilerParams(
             collective_id=0, has_side_effects=True, vmem_limit_bytes=60 << 20

time: 306 us -> 293 us (0.958)
  Pallas kernels: 301 us -> 288 us
    pallas_call x1, Pallas kernels: 301 us -> 288 us  [relay(): pl.pallas_call(functools.partial(relay_kernel, sections, columns), out_sh...]
where the time goes in v6:
time: 293 us
  Pallas kernels  288 us (98%)
    pallas_call x1, Pallas kernels, relay(): pl.pallas_call(functools.partial(relay_kernel, sections, columns), out_sh...  288 us

profile of v6, /device:TPU:1, one launch (start us, length us, event | category | flops | bytes accessed | tf_op | source)
XLA Modules:
  0.0 293.1 jit_solution(9719122070131131818)
XLA Ops:
  0.0 0.0 copy-start
  0.0 1.3 fusion.5
  1.3 0.0 copy-done
  1.3 0.1 copy.12
  1.5 0.1 fusion.4
  1.6 0.0 copy-start.1
  1.6 1.2 pad_maximum_fusion.wcat_ref
  2.8 0.0 copy-done.1
  2.8 0.6 broadcast_in_dim.3.embed_ref
  3.3 288.2 %shard_map.82 = f32[4,32,1]{2,1,0:T(8,128)} custom-call(bf16[4,256,1536]{2,1,0:T(8,128)(2,1)} %bitcast.16, bf16[2,2,96,1664]{3,2,1,0:T(8,128)(2,1)} %pad_maximum_fusion.wcat_ref, bf16[1536,768]{1,0:T(8,128)(2,1)} %wctx_hbm.1, bf16[1536,768]{1,0:T(8,128)(2,1)} %wtgt_hbm.1, bf16[1,1536]{1,0:T(2,128)(2,1)} %broadcast_in_dim.3.embed_ref, s32[4,12]{1,0:T(4,128)} %bitcast.20, ...), custom_call_target="tpu_custom_call" | custom-call | tf_op jit(solution)/shard_map/pallas_call | solution.py:538
  291.6 1.5 reduce
Async XLA Ops:
  0.0 1.3 copy-start
  1.6 1.2 copy-start.1

commit v7 on v6

--- a/solution.py
+++ b/solution.py
@@ -57,6 +57,7 @@
     _, utts, _, frames, half = xall.shape
     micro = utts // CORES
     mine = half // CW
+    sent = half // LANES
     width = half * CORES
     share = frames // sections
     last = sections - 1
@@ -291,7 +292,7 @@
     prepare(0)
 
     def piece(a, i, c, j):
-        return xall.at[a, i, c, :, pl.ds(j * CW, CW)]
+        return xall.at[a, i, c, :, pl.ds(j * LANES, LANES)]
 
     def hop(i, j):
         return remote(
@@ -308,7 +309,7 @@
         return remote(at, at, swap_send.at[a, i, j], swap_recv.at[a, i, j], s, peer)
 
     def swap_in(a, i):
-        for j in range(mine):
+        for j in range(sent):
             swap(a, i, j, 1 - core).wait_recv()
 
     def scatter(i, j):
@@ -345,7 +346,7 @@
 
             @pl.when((s > 0) & (a == 0))
             def _():
-                for j in range(mine):
+                for j in range(sent):
                     hop(i, j).wait_recv()
                     swap(0, i, j, core).start()
 
@@ -421,13 +422,13 @@
                             kept + mixed * jax.nn.sigmoid(mixed)
                         ).astype(jnp.bfloat16)
 
-                @pl.when(a == 0)
-                def _():
-                    swap(1, i, j, core).start()
-
-                @pl.when((a == 1) & (s < last))
-                def _():
-                    hop(i, j).start()
+                    @pl.when(a == 0)
+                    def _():
+                        swap(1, i, j * (CW // LANES) + h, core).start()
+
+                    @pl.when((a == 1) & (s < last))
+                    def _():
+                        hop(i, j * (CW // LANES) + h).start()
 
                 return carry
 
@@ -498,7 +499,7 @@
             init(m).wait_send()
 
     def drain(i, carry):
-        for j in range(mine):
+        for j in range(sent):
             swap(1, i, j, core).wait_send()
 
             @pl.when(s < last)
@@ -560,10 +561,10 @@
             dma((2, 7, CORES)),
             dma((micro,)),
             dma((micro,)),
-            dma((utts, mine)),
-            dma((utts, mine)),
-            dma((2, utts, mine)),
-            dma((2, utts, mine)),
+            dma((utts, half // LANES)),
+            dma((utts, half // LANES)),
+            dma((2, utts, half // LANES)),
+            dma((2, utts, half // LANES)),
             dma((utts, sections)),
             dma((micro, CORES)),
         ],

time: 293 us -> 289 us (0.986)
  Pallas kernels: 288 us -> 284 us
    pallas_call x1, Pallas kernels: 288 us -> 284 us  [relay(): pl.pallas_call(functools.partial(relay_kernel, sections, columns), out_sh...]
where the time goes in v7:
time: 289 us
  Pallas kernels  284 us (98%)
    pallas_call x1, Pallas kernels, relay(): pl.pallas_call(functools.partial(relay_kernel, sections, columns), out_sh...  284 us

profile of v7, /device:TPU:1, one launch (start us, length us, event | category | flops | bytes accessed | tf_op | source)
XLA Modules:
  0.0 289.0 jit_solution(17597273924444220033)
XLA Ops:
  0.0 0.0 copy-start
  0.0 1.3 fusion.5
  1.3 0.0 copy-done
  1.3 0.1 copy.12
  1.5 0.1 fusion.4
  1.6 0.0 copy-start.1
  1.6 1.2 pad_maximum_fusion.wcat_ref
  2.8 0.0 copy-done.1
  2.8 0.6 broadcast_in_dim.3.embed_ref
  3.3 284.1 %shard_map.82 = f32[4,32,1]{2,1,0:T(8,128)} custom-call(bf16[4,256,1536]{2,1,0:T(8,128)(2,1)} %bitcast.16, bf16[2,2,96,1664]{3,2,1,0:T(8,128)(2,1)} %pad_maximum_fusion.wcat_ref, bf16[1536,768]{1,0:T(8,128)(2,1)} %wctx_hbm.1, bf16[1536,768]{1,0:T(8,128)(2,1)} %wtgt_hbm.1, bf16[1,1536]{1,0:T(2,128)(2,1)} %broadcast_in_dim.3.embed_ref, s32[4,12]{1,0:T(4,128)} %bitcast.20, ...), custom_call_target="tpu_custom_call" | custom-call | tf_op jit(solution)/shard_map/pallas_call | solution.py:539
  287.4 1.5 reduce
Async XLA Ops:
  0.0 1.3 copy-start
  1.6 1.2 copy-start.1

commit v8 on v7

--- a/solution.py
+++ b/solution.py
@@ -21,7 +21,8 @@
     sections,
     columns,
     feats_hbm,
-    wcat_ref,
+    w_hbm,
+    taps_hbm,
     wctx_hbm,
     wtgt_hbm,
     embed_ref,
@@ -110,32 +111,32 @@
     def rows_of(column):
         return pl.ds(pl.multiple_of(column * rows, 32), rows)
 
-    def own_out(t, h):
+    def own_parts(t, h, a, at):
+        low_half, high_half = slice(0, half), slice(half, 2 * half)
+        return (
+            (w_hbm.at[t, :, h * half : (h + 1) * half], wv.at[a, at, low_half]),
+            (w_hbm.at[t, :, width + h * half : width + (h + 1) * half], wv.at[a, at, high_half]),
+            (taps_hbm.at[t], wv.at[a, at, 2 * half : 2 * half + LANES]),
+        )
+
+    def own_out(t, h, p):
+        src, dst = own_parts(t, h, lax.rem(s, 2), rows_of(f))[p]
         return remote(
-            wcat_ref.at[t, h],
-            wv.at[lax.rem(s, 2), rows_of(f)],
-            own_send.at[t, h],
-            own_recv.at[lax.rem(s, 2), core],
+            src,
+            dst,
+            own_send.at[t, h, p],
+            own_recv.at[lax.rem(s, 2), core, p],
             s // 2 + (sections // 2) * t,
             f - core + h,
         )
 
-    def own_here(t, h):
-        return pltpu.make_async_copy(
-            wcat_ref.at[t, h],
-            wv.at[lax.rem(s, 2), rows_of(f)],
-            own_recv.at[lax.rem(s, 2), core],
-        )
-
-    def own_in(a, c):
-        return remote(
-            wcat_ref.at[0, 0],
-            wv.at[a, rows_of(f - core + c)],
-            own_send.at[0, 0],
-            own_recv.at[a, c],
-            s,
-            peer,
-        )
+    def own_here(t, h, p):
+        src, dst = own_parts(t, h, lax.rem(s, 2), rows_of(f))[p]
+        return pltpu.make_async_copy(src, dst, own_recv.at[lax.rem(s, 2), core, p])
+
+    def own_in(a, c, p):
+        src, dst = own_parts(0, 0, a, rows_of(f - core + c))[p]
+        return remote(src, dst, own_send.at[0, 0, p], own_recv.at[a, c, p], s, peer)
 
     stays = [(s == 0), (s == last)]
 
@@ -145,11 +146,13 @@
 
             @pl.when(here)
             def _():
-                own_here(t, h).start()
+                for p in range(3):
+                    own_here(t, h, p).start()
 
             @pl.when(jnp.logical_not(here))
             def _():
-                own_out(t, h).start()
+                for p in range(3):
+                    own_out(t, h, p).start()
 
     send_own(0)
     send_own(1)
@@ -194,11 +197,13 @@
 
             @pl.when(here)
             def _():
-                own_here(a, u).wait()
+                for p in range(3):
+                    own_here(a, u, p).wait()
 
             @pl.when(jnp.logical_not(here))
             def _():
-                own_in(a, u).wait_recv()
+                for p in range(3):
+                    own_in(a, u, p).wait_recv()
 
             for n in (0, 1, 2):
                 ring_out(a, n, u).start()
@@ -476,7 +481,11 @@
         )
         positive = jnp.sum(jnp.where(spots == rows_at, sims, 0.0), axis=1, keepdims=True)
         negative = jnp.sum(cnt[m] * jnp.exp(sims), axis=1, keepdims=True)
-        out_ref[m] = jnp.log(jnp.exp(positive) + negative) - positive
+        loss = jnp.log(jnp.exp(positive) + negative) - positive
+        across_row = lax.broadcasted_iota(jnp.int32, (share, share), 1)
+        down_row = lax.broadcasted_iota(jnp.int32, (share, share), 0)
+        on_diagonal = jnp.where(across_row == down_row, loss, 0.0)
+        out_ref[pl.ds(m, 1), :] = jnp.sum(on_diagonal, axis=0, keepdims=True)
         return carry
 
     lax.fori_loop(0, micro, score, 0)
@@ -486,7 +495,8 @@
 
             @pl.when(jnp.logical_not(stays[t] & (core == h)))
             def _():
-                own_out(t, h).wait_send()
+                for p in range(3):
+                    own_out(t, h, p).wait_send()
 
     for a in range(2):
         for n in range(7):
@@ -524,7 +534,7 @@
     lax.fori_loop(0, utts, drain, 0)
 
 
-def relay(sections, columns, feats, wcat, w_ctx, w_tgt, embed, starts, picks):
+def relay(sections, columns, feats, w_in, taps, w_ctx, w_tgt, embed, starts, picks):
     micro, frames, width = feats.shape
     share = frames // sections
     proj = w_ctx.shape[1]
@@ -538,8 +548,8 @@
     bf16 = jnp.bfloat16
     return pl.pallas_call(
         functools.partial(relay_kernel, sections, columns),
-        out_shape=jax.ShapeDtypeStruct((micro, share, 1), jnp.float32),
-        in_specs=[hbm, hbm, hbm, hbm, vmem, smem, vmem],
+        out_shape=jax.ShapeDtypeStruct((micro, share), jnp.float32),
+        in_specs=[hbm, hbm, hbm, hbm, hbm, vmem, smem, vmem],
         out_specs=vmem,
         scratch_shapes=[
             pltpu.VMEM(feats.shape, bf16),
@@ -550,13 +560,13 @@
             pltpu.VMEM((mine, 2, frames, CW), jnp.float32),
             pltpu.VMEM((CW // LANES, frames + 2 * PAD, LANES), jnp.float32),
             pltpu.VMEM((2, 8, 2 * half), jnp.float32),
-            pltpu.VMEM((2, width, wcat.shape[3]), bf16),
+            pltpu.VMEM((2, width, 2 * half + LANES), bf16),
             pltpu.VMEM((2, half // LANES, 32, LANES), jnp.float32),
             pltpu.VMEM((micro, frames, proj), bf16),
             pltpu.VMEM((micro, share, frames), jnp.float32),
             pltpu.VMEM((micro, CORES, share, half), bf16),
-            dma((2, CORES)),
-            dma((2, CORES)),
+            dma((2, CORES, 3)),
+            dma((2, CORES, 3)),
             dma((2, 7, CORES)),
             dma((2, 7, CORES)),
             dma((micro,)),
@@ -571,44 +581,28 @@
         compiler_params=pltpu.CompilerParams(
             collective_id=0, has_side_effects=True, vmem_limit_bytes=60 << 20
         ),
-    )(feats, wcat, w_ctx, w_tgt, embed, starts, picks)
+    )(feats, w_in, taps, w_ctx, w_tgt, embed, starts, picks)
 
 
 def on_device(feats, w_in, dw_kernel, mask_embed, w_ctx, w_tgt, mask_starts, distractors):
     sections = lax.axis_size("section")
     columns = lax.axis_size("fsdp")
-    width = feats.shape[3]
-    half = width // CORES
 
     taps = dw_kernel[:, 0].transpose(0, 2, 1)
     taps = jnp.pad(taps, ((0, 0), (0, 0), (0, LANES - taps.shape[2])))
-    rows = w_in[:, 0]
-    wcat = jnp.stack(
-        [
-            jnp.concatenate(
-                [
-                    rows[:, :, h * half : (h + 1) * half],
-                    rows[:, :, width + h * half : width + (h + 1) * half],
-                    taps,
-                ],
-                axis=2,
-            )
-            for h in range(CORES)
-        ],
-        axis=1,
-    )
     loss = relay(
         sections,
         columns,
         feats[:, 0],
-        wcat,
+        w_in[:, 0],
+        taps,
         w_ctx,
         w_tgt,
         mask_embed[None, :],
         mask_starts[:, 0],
         distractors[:, 0],
     )
-    return loss[:, :, 0][:, None, :]
+    return loss[:, None, :]
 
 
 def solution(mesh):

time: 289 us -> 288 us (level)
  no operation moved by 1% of the time
where the time goes in v8:
time: 288 us
  Pallas kernels  284 us (99%)
  local copies, waits for them, and re-layouts  3.99 us (1%)
    pallas_call x1, Pallas kernels, relay(): pl.pallas_call(functools.partial(relay_kernel, sections, columns), out_sh...  284 us

profile of v8, /device:TPU:1, one launch (start us, length us, event | category | flops | bytes accessed | tf_op | source)
XLA Modules:
  0.0 287.7 jit_solution(12827830148333674161)
XLA Ops:
  0.0 0.8 copy.9
  0.8 0.6 pad.4.taps_hbm
  1.5 1.3 broadcast_in_dim.6.embed_ref
  2.8 283.7 %shard_map.82 = f32[4,32]{1,0:T(4,128)} custom-call(bf16[4,256,1536]{2,1,0:T(8,128)(2,1)} %bitcast.10, bf16[2,96,3072]{2,1,0:T(8,128)(2,1)} %bitcast.11, bf16[2,96,128]{2,1,0:T(8,128)(2,1)} %pad.4.taps_hbm, bf16[1536,768]{1,0:T(8,128)(2,1)} %wctx_hbm.1, bf16[1536,768]{1,0:T(8,128)(2,1)} %wtgt_hbm.1, bf16[1,1536]{1,0:T(2,128)(2,1)} %broadcast_in_dim.6.embed_ref, ...), custom_call_target="tpu_custom_call" | custom-call | tf_op jit(solution)/shard_map/pallas_call | solution.py:549
  286.5 1.2 copy.12
